TPU v7x, 32 devices: a whole 2x2x4 slice. The times are simulated.
32 devices in a mesh: groups: 2 (over y), blocks: 8 (over z, x), inst: 2 (over core).
Axes of the slice: x: 2, y: 2, z: 4, core: 2. Of those that a mesh axis runs over, the one named last changes fastest.
Arguments:
- adjoint_start: float32 [32, 6, 16, 8, 128], P(('groups', 'inst'), None, 'blocks'), parts along dimension 0, may hold values from -6 to 6
- objective_grad: float32 [32, 6, 16, 8, 128], P(('groups', 'inst'), None, 'blocks'), parts along dimension 0, may hold values from -6 to 6
- diag_inverse: float32 [32, 6, 6, 16, 8, 128], P(('groups', 'inst'), None, None, 'blocks'), parts along dimension 0, may hold values from -0.1 to 0.5, as said below
- face_coupling: float32 [32, 6, 16, 8, 128], P(('groups', 'inst'), None, 'blocks'), parts along dimension 0, may hold values from 0.05 to 0.5
- surface_index: int32 [4096], P(('groups', 'blocks')), parts along dimension 0, may hold values from 0 to 2047
- wall_point_partials: float32 [32, 3, 6, 2048], P(('groups', 'inst'), None, None, 'blocks'), parts along dimension 0, may hold values from -0.625 to 0.625
Outputs:
- adjoint: float32 [32, 6, 16, 8, 128], P(('groups', 'inst'), None, 'blocks'), parts along dimension 0
- sensitivity: float32 [3, 4096], P(None, ('groups', 'blocks')), parts along dimension 1
There are 2 independent parts, one for each index of `groups`. A program takes and returns all parts, laid end to end along the dimension named above; each array names one. Nothing has to cross between parts.
Inputs may be any that keep to these rules, and one draw needn't show every extreme that they name: `surface_index`: each entry is a cell of its own block. `diag_inverse`: each 6 x 6 block has diagonal entries between 0.25 and 0.5.
All inputs are finite; a program needn't handle non-finite values.
Results may differ from a plain program's by a relative error of at most 0.0001.
Values sent between devices are 32-bit elements; how exact they have to be, the bound alone decides.
No kernel may reach another device: no remote copies, remote signals or barrier semaphores. Data moves between devices by JAX's collectives and lax.ppermute only.
A program may use at most 64 MiB of HBM per device.

v0:
```python
import jax
import jax.numpy as jnp
from jax import lax
from jax.sharding import PartitionSpec as P

SWEEPS = 4


spectral_weight = 0.25


def extended(cells, sides, width):
    for axis, dim in sides:
        count = lax.axis_size(axis)
        head = lax.slice_in_dim(cells, 0, width, axis=dim)
        tail = lax.slice_in_dim(cells, cells.shape[dim] - width, cells.shape[dim], axis=dim)
        cells = jnp.concatenate(
            [
                lax.ppermute(tail, axis, [(i, (i + 1) % count) for i in range(count)]),
                cells,
                lax.ppermute(head, axis, [((i + 1) % count, i) for i in range(count)]),
            ],
            axis=dim,
        )
    return cells


def spectral_matrix(number):
    indices = jnp.arange(number, dtype=jnp.int32)
    distance = (indices[:, None] - indices[None, :]) % number
    angle = jnp.pi * distance.astype(jnp.float32) / number
    color_parity = (1 - 2 * (distance % 2)).astype(jnp.float32)
    sine = jnp.where(distance == 0, jnp.float32(1.0), jnp.sin(angle))
    value_entries = jnp.where(
        distance == 0, jnp.float32(0.0), 0.5 * color_parity * jnp.cos(angle) / sine
    )
    return value_entries * spectral_weight


def displace(field, mesh_axis_count, amount):
    widths = [(0, 0)] * field.ndim
    length = field.shape[mesh_axis_count]
    if amount > 0:
        widths[mesh_axis_count] = (1, 0)
        padded = jnp.pad(field, widths)
        return lax.slice_in_dim(padded, 0, length, axis=mesh_axis_count)
    widths[mesh_axis_count] = (0, 1)
    padded = jnp.pad(field, widths)
    return lax.slice_in_dim(padded, 1, length + 1, axis=mesh_axis_count)


def neighbours(center, below, above, coupling):
    total = coupling[:, 0:1] * below + coupling[:, 1:2] * above
    total = (
        total
        + coupling[:, 2:3] * displace(center, 3, 1)
        + coupling[:, 3:4] * displace(center, 3, -1)
    )
    total = (
        total
        + coupling[:, 4:5] * displace(center, 4, 1)
        + coupling[:, 5:6] * displace(center, 4, -1)
    )
    return total


def sweep_update(objective_grad, diag_inverse, coupled_terms, spectral_term):
    resid = objective_grad + coupled_terms - spectral_term
    return jnp.einsum("nuvira,nuira->nvira", diag_inverse, resid, precision=lax.Precision.HIGHEST)


def body(
    adjoint_start, objective_grad, diag_inverse, face_coupling, surface_index, wall_point_partials
):
    inst_dev = adjoint_start.shape[0]
    number = inst_dev * lax.axis_size("inst")
    spectral = spectral_matrix(number)
    first = lax.axis_index("inst") * inst_dev
    adjoint = adjoint_start
    for repeat in range(SWEEPS):
        padded = extended(adjoint, (("blocks", 2),), 1)
        below = padded[:, :, :-2]
        above = padded[:, :, 2:]
        coupled_terms = neighbours(adjoint, below, above, face_coupling)
        current = adjoint
        own_columns = lax.dynamic_slice_in_dim(spectral, first, inst_dev, 1)
        spectral_term = jnp.einsum(
            "mn,mvira->nvira",
            own_columns,
            lax.all_gather(current, "inst", axis=0, tiled=True),
            precision=lax.Precision.HIGHEST,
        )
        adjoint = sweep_update(objective_grad, diag_inverse, coupled_terms, spectral_term)
    flat_vector = adjoint.reshape(inst_dev, adjoint.shape[1], -1)
    selected_entries = jnp.take(flat_vector, surface_index, axis=2)
    local_terms = jnp.einsum(
        "fex,fpex->px", selected_entries, wall_point_partials, precision=lax.Precision.HIGHEST
    )
    sensitivity = lax.psum(local_terms, "inst")
    return (adjoint, sensitivity)


def solution(mesh):
    return jax.shard_map(
        body,
        mesh=mesh,
        in_specs=(
            P(("groups", "inst"), None, "blocks", None, None),
            P(("groups", "inst"), None, "blocks", None, None),
            P(("groups", "inst"), None, None, "blocks", None, None),
            P(("groups", "inst"), None, "blocks", None, None),
            P(("groups", "blocks")),
            P(("groups", "inst"), None, None, "blocks"),
        ),
        out_specs=(
            P(("groups", "inst"), None, "blocks", None, None),
            P(None, ("groups", "blocks")),
        ),
        check_vma=False,
    )
```

profile of v0, /device:TPU:0, one launch (start us, length us, event | category | flops | bytes accessed | tf_op | source)
XLA Modules:
  0.0 71.4 jit_solution(15422257214266357655)
XLA Ops:
  0.6 0.0 copy-start.2
  0.6 0.0 copy-start.4
  0.6 1.3 %copy.11 = f32[8,6,2,8,128]{4,0,3,2,1:T(8,128)S(1)} copy(f32[8,6,2,8,128]{4,3,2,1,0:T(8,128)} %param.6) | data formatting | bytes 786432 | tf_op args[0]
  2.0 3.0 %collective-permute-start = (f32[8,6,1,8,128]{4,0,3,2,1:T(8,128)S(1)}, f32[8,6,1,8,128]{4,0,3,2,1:T(8,128)S(1)}, u32[]{:S(2)}, u32[]{:S(2)}) collective-permute-start(f32[8,6,1,8,128]{4,0,3,2,1:T(8,128)S(1)} %get-tuple-element.14), channel_id=1, source_target_pairs={{0,2},{2,4},{4,6},{6,8},{8,10},{10,12},{12,14},{14,0},{1,3},{3,5},... | collective-permute-start | bytes 589832 | tf_op jit(solution)/shard_map/ppermute | solution.py:19
  5.0 3.1 %collective-permute-start.1 = (f32[8,6,1,8,128]{4,0,3,2,1:T(8,128)S(1)}, f32[8,6,1,8,128]{4,0,3,2,1:T(8,128)S(1)}, u32[]{:S(2)}, u32[]{:S(2)}) collective-permute-start(f32[8,6,1,8,128]{4,0,3,2,1:T(8,128)S(1)} %get-tuple-element.15), channel_id=1, source_target_pairs={{2,0},{4,2},{6,4},{8,6},{10,8},{12,10},{14,12},{0,14},{3,1},{5,3},... | collective-permute-start | bytes 589832 | tf_op jit(solution)/shard_map/ppermute | solution.py:21
  8.1 0.7 compare_select_fusion
  8.8 0.7 compare_and_fusion
  9.5 1.0 %slice_bitcast_fusion.5 = (f32[8,2,8,128]{3,2,1,0:T(8,128)S(1)}, f32[8,2,8,128]{3,2,1,0:T(8,128)S(1)}, f32[8,2,8,128]{3,2,1,0:T(8,128)S(1)}, f32[8,2,8,128]{3,2,...) fusion(f32[8,6,2,8,128]{4,3,2,1,0:T(8,128)} %param.9), kind=kLoop, calls=%fused_computation.99 | loop fusion | bytes 786432 | tf_op jit(solution)/shard_map/mul | solution.py:53
  10.7 0.1 fusion.68
  10.8 0.0 copy-done.2
  10.8 0.0 copy-start
  10.8 2.5 %all_gather.12 = f32[16,6,2,8,128]{4,3,2,1,0:T(8,128)S(1)} all-gather(f32[8,6,2,8,128]{4,3,2,1,0:T(8,128)S(1)} %copy-done.2), channel_id=1, replica_groups=mesh['groups'=2,'blocks'=8,'inst'=2] {'inst'}, dimensions={0}, use_global_device_ids=true | all-gather | bytes 1179648 | tf_op jit(solution)/shard_map/all_gather | solution.py:90
  13.3 0.0 collective-permute-done
  13.3 2.2 %collective-permute-done.1 = f32[8,6,1,8,128]{4,0,3,2,1:T(8,128)S(1)} collective-permute-done((f32[8,6,1,8,128]{4,0,3,2,1:T(8,128)S(1)}, f32[8,6,1,8,128]{4,0,3,2,1:T(8,128)S(1)}, u32[]{:S(2)}, u32[]{:S(2)}) %collective-permute-start.1) | collective-permute-done | bytes 196640 | tf_op jit(solution)/shard_map/ppermute | solution.py:21
  15.6 0.0 copy-done.4
  15.6 1.3 %fusion.3 = f32[8,2,8,128,6]{3,0,2,1,4:T(8,128)S(1)} fusion(f32[16,8,1,1,1]{0,1,4,3,2:T(8,128)S(1)} %fusion.68, f32[16,6,2,8,128]{4,3,2,1,0:T(8,128)S(1)} %all_gather.12, f32[8,6,2,8,128]{4,0,3,2,1:T(8,128)S(1)} %copy.11, f32[8,6,1,8,128]{4,0,3,2,1:T(8,128)S(1)} %collective-permute-done.1, f32[8,6,1,8,128]{4,0,3,2,1:T(8,128)S(1)} %collective-permute-done, ...), kind=kOutput, calls=%fused_computation.12 | convolution fusion | flops 20348928 | bytes 2753024 | tf_op jit(solution)/shard_map/mn,mvira->nvira/dot_general | solution.py:87
  16.8 0.1 copy.82
  16.9 0.0 copy-done
  16.9 0.3 multiply_reduce_fusion.3
  17.3 0.2 copy.109
  17.5 0.3 collective-permute-start.2
  17.9 4.4 %collective-permute-start.3 = (f32[8,6,1,8,128]{4,0,3,2,1:T(8,128)S(1)}, f32[8,6,1,8,128]{4,0,3,2,1:T(8,128)S(1)}, u32[]{:S(2)}, u32[]{:S(2)}) collective-permute-start(f32[8,6,1,8,128]{4,0,3,2,1:T(8,128)S(1)} %get-tuple-element.7), channel_id=1, source_target_pairs={{2,0},{4,2},{6,4},{8,6},{10,8},{12,10},{14,12},{0,14},{3,1},{5,3},... | collective-permute-start | bytes 589832 | tf_op jit(solution)/shard_map/ppermute | solution.py:21
  22.3 2.4 %all_gather.13 = f32[16,6,2,8,128]{4,3,2,1,0:T(8,128)S(1)} all-gather(f32[8,6,2,8,128]{4,3,2,1,0:T(8,128)S(1)} %bitcast.58), channel_id=1, replica_groups=mesh['groups'=2,'blocks'=8,'inst'=2] {'inst'}, dimensions={0}, use_global_device_ids=true | all-gather | bytes 1179648 | tf_op jit(solution)/shard_map/all_gather | solution.py:90
  24.7 1.3 %collective-permute-done.2 = f32[8,6,1,8,128]{4,0,3,2,1:T(8,128)S(1)} collective-permute-done((f32[8,6,1,8,128]{4,0,3,2,1:T(8,128)S(1)}, f32[8,6,1,8,128]{4,0,3,2,1:T(8,128)S(1)}, u32[]{:S(2)}, u32[]{:S(2)}) %collective-permute-start.2) | collective-permute-done | bytes 196640 | tf_op jit(solution)/shard_map/ppermute | solution.py:19
  26.0 3.3 %collective-permute-done.3 = f32[8,6,1,8,128]{4,0,3,2,1:T(8,128)S(1)} collective-permute-done((f32[8,6,1,8,128]{4,0,3,2,1:T(8,128)S(1)}, f32[8,6,1,8,128]{4,0,3,2,1:T(8,128)S(1)}, u32[]{:S(2)}, u32[]{:S(2)}) %collective-permute-start.3) | collective-permute-done | bytes 196640 | tf_op jit(solution)/shard_map/ppermute | solution.py:21
  29.3 1.3 %fusion.2 = f32[8,2,8,128,6]{3,0,2,1,4:T(8,128)S(1)} fusion(f32[16,8,1,1,1]{0,1,4,3,2:T(8,128)S(1)} %fusion.68, f32[16,6,2,8,128]{4,3,2,1,0:T(8,128)S(1)} %all_gather.13, f32[8,6,2,8,128]{4,0,3,2,1:T(8,128)S(1)} %bitcast.66, f32[8,6,1,8,128]{4,0,3,2,1:T(8,128)S(1)} %collective-permute-done.3, f32[8,6,1,8,128]{4,0,3,2,1:T(8,128)S(1)} %collective-permute-done.2, ...), kind=kOutput, calls=%fused_computation.10 | convolution fusion | flops 20348928 | bytes 2753024 | tf_op jit(solution)/shard_map/mn,mvira->nvira/dot_general | solution.py:87
  30.6 0.1 copy.83
  30.7 0.3 multiply_reduce_fusion.2
  31.0 0.2 copy.108
  31.3 0.1 collective-permute-start.4
  31.4 4.7 %collective-permute-start.5 = (f32[8,6,1,8,128]{4,0,3,2,1:T(8,128)S(1)}, f32[8,6,1,8,128]{4,0,3,2,1:T(8,128)S(1)}, u32[]{:S(2)}, u32[]{:S(2)}) collective-permute-start(f32[8,6,1,8,128]{4,0,3,2,1:T(8,128)S(1)} %get-tuple-element.5), channel_id=1, source_target_pairs={{2,0},{4,2},{6,4},{8,6},{10,8},{12,10},{14,12},{0,14},{3,1},{5,3},... | collective-permute-start | bytes 589832 | tf_op jit(solution)/shard_map/ppermute | solution.py:21
  36.1 2.4 %all_gather.14 = f32[16,6,2,8,128]{4,3,2,1,0:T(8,128)S(1)} all-gather(f32[8,6,2,8,128]{4,3,2,1,0:T(8,128)S(1)} %bitcast.59), channel_id=1, replica_groups=mesh['groups'=2,'blocks'=8,'inst'=2] {'inst'}, dimensions={0}, use_global_device_ids=true | all-gather | bytes 1179648 | tf_op jit(solution)/shard_map/all_gather | solution.py:90
  38.4 1.9 %collective-permute-done.4 = f32[8,6,1,8,128]{4,0,3,2,1:T(8,128)S(1)} collective-permute-done((f32[8,6,1,8,128]{4,0,3,2,1:T(8,128)S(1)}, f32[8,6,1,8,128]{4,0,3,2,1:T(8,128)S(1)}, u32[]{:S(2)}, u32[]{:S(2)}) %collective-permute-start.4) | collective-permute-done | bytes 196640 | tf_op jit(solution)/shard_map/ppermute | solution.py:19
  40.4 2.9 %collective-permute-done.5 = f32[8,6,1,8,128]{4,0,3,2,1:T(8,128)S(1)} collective-permute-done((f32[8,6,1,8,128]{4,0,3,2,1:T(8,128)S(1)}, f32[8,6,1,8,128]{4,0,3,2,1:T(8,128)S(1)}, u32[]{:S(2)}, u32[]{:S(2)}) %collective-permute-start.5) | collective-permute-done | bytes 196640 | tf_op jit(solution)/shard_map/ppermute | solution.py:21
  43.3 1.3 %fusion.1 = f32[8,2,8,128,6]{3,0,2,1,4:T(8,128)S(1)} fusion(f32[16,8,1,1,1]{0,1,4,3,2:T(8,128)S(1)} %fusion.68, f32[16,6,2,8,128]{4,3,2,1,0:T(8,128)S(1)} %all_gather.14, f32[8,6,2,8,128]{4,0,3,2,1:T(8,128)S(1)} %bitcast.68, f32[8,6,1,8,128]{4,0,3,2,1:T(8,128)S(1)} %collective-permute-done.5, f32[8,6,1,8,128]{4,0,3,2,1:T(8,128)S(1)} %collective-permute-done.4, ...), kind=kOutput, calls=%fused_computation.8 | convolution fusion | flops 20348928 | bytes 2753024 | tf_op jit(solution)/shard_map/mn,mvira->nvira/dot_general | solution.py:87
  44.6 0.1 copy.84
  44.6 0.3 multiply_reduce_fusion.1
  45.0 0.2 copy.107
  45.2 0.1 collective-permute-start.6
  45.3 4.7 %collective-permute-start.7 = (f32[8,6,1,8,128]{4,0,3,2,1:T(8,128)S(1)}, f32[8,6,1,8,128]{4,0,3,2,1:T(8,128)S(1)}, u32[]{:S(2)}, u32[]{:S(2)}) collective-permute-start(f32[8,6,1,8,128]{4,0,3,2,1:T(8,128)S(1)} %get-tuple-element.3), channel_id=1, source_target_pairs={{2,0},{4,2},{6,4},{8,6},{10,8},{12,10},{14,12},{0,14},{3,1},{5,3},... | collective-permute-start | bytes 589832 | tf_op jit(solution)/shard_map/ppermute | solution.py:21
  50.0 2.4 %all_gather.15 = f32[16,6,2,8,128]{4,3,2,1,0:T(8,128)S(1)} all-gather(f32[8,6,2,8,128]{4,3,2,1,0:T(8,128)S(1)} %bitcast.60), channel_id=1, replica_groups=mesh['groups'=2,'blocks'=8,'inst'=2] {'inst'}, dimensions={0}, use_global_device_ids=true | all-gather | bytes 1179648 | tf_op jit(solution)/shard_map/all_gather | solution.py:90
  52.4 1.7 %collective-permute-done.6 = f32[8,6,1,8,128]{4,0,3,2,1:T(8,128)S(1)} collective-permute-done((f32[8,6,1,8,128]{4,0,3,2,1:T(8,128)S(1)}, f32[8,6,1,8,128]{4,0,3,2,1:T(8,128)S(1)}, u32[]{:S(2)}, u32[]{:S(2)}) %collective-permute-start.6) | collective-permute-done | bytes 196640 | tf_op jit(solution)/shard_map/ppermute | solution.py:19
  54.1 3.2 %collective-permute-done.7 = f32[8,6,1,8,128]{4,0,3,2,1:T(8,128)S(1)} collective-permute-done((f32[8,6,1,8,128]{4,0,3,2,1:T(8,128)S(1)}, f32[8,6,1,8,128]{4,0,3,2,1:T(8,128)S(1)}, u32[]{:S(2)}, u32[]{:S(2)}) %collective-permute-start.7) | collective-permute-done | bytes 196640 | tf_op jit(solution)/shard_map/ppermute | solution.py:21
  57.2 1.3 %fusion = f32[8,2,8,128,6]{3,0,2,1,4:T(8,128)S(1)} fusion(f32[16,8,1,1,1]{0,1,4,3,2:T(8,128)S(1)} %fusion.68, f32[16,6,2,8,128]{4,3,2,1,0:T(8,128)S(1)} %all_gather.15, f32[8,6,2,8,128]{4,0,3,2,1:T(8,128)S(1)} %bitcast.64, f32[8,6,1,8,128]{4,0,3,2,1:T(8,128)S(1)} %collective-permute-done.7, f32[8,6,1,8,128]{4,0,3,2,1:T(8,128)S(1)} %collective-permute-done.6, ...), kind=kOutput, calls=%fused_computation.6 | convolution fusion | flops 20348928 | bytes 2753024 | tf_op jit(solution)/shard_map/mn,mvira->nvira/dot_general | solution.py:87
  58.5 0.1 copy.85
  58.6 0.3 multiply_reduce_fusion
  58.9 0.0 copy-start.1
  58.9 4.4 %copy.81 = f32[8,6,2,8,128]{1,0,4,3,2:T(8,128)} copy(f32[8,6,2,8,128]{4,3,2,1,0:T(8,128)S(1)} %bitcast.61) | data formatting | bytes 786432 | tf_op jit(solution)/shard_map/reshape | solution.py:94
  63.4 0.0 copy-done.1
  63.4 0.0 copy-start.3
  63.4 4.2 %gather_fusion = f32[256,8,6]{2,1,0:T(8,128)S(1)} fusion(f32[8,6,2048]{1,0,2:T(8,128)} %bitcast.57, s32[1024]{0:T(1024)S(1)} %pad_clamp_fusion), kind=kCustom, calls=%fused_computation | custom fusion | bytes 99328 | tf_op jit(solution)/shard_map/jit(_take)/gather | solution.py:95
  67.5 0.3 select_bitcast_fusion
  67.9 0.4 copy.86
  68.3 0.0 copy-done.3
  68.3 3.1 %psum.7 = f32[3,256]{1,0:T(4,128)} all-reduce(f32[3,256]{1,0:T(4,128)S(1)} %bitcast.69), channel_id=1, replica_groups=mesh['groups'=2,'blocks'=8,'inst'=2] {'inst'}, use_global_device_ids=true, to_apply=%region_0.1 | all-reduce | flops 768 | bytes 6144 | tf_op jit(solution)/shard_map/psum | solution.py:99
  (14 shorter events, 0.3 us)
Async XLA Ops:
  0.6 10.2 %copy-start.2 = (f32[8,6,2,8,128]{4,3,2,1,0:T(8,128)S(1)}, f32[8,6,2,8,128]{4,3,2,1,0:T(8,128)}, u32[]{:S(2)}) copy-start(f32[8,6,2,8,128]{4,3,2,1,0:T(8,128)} %param.6) | copy-start | bytes 1179652
  0.6 14.9 %copy-start.4 = (f32[8,6,2,8,128]{4,3,2,1,0:T(8,128)S(1)}, f32[8,6,2,8,128]{4,3,2,1,0:T(8,128)}, u32[]{:S(2)}) copy-start(f32[8,6,2,8,128]{4,3,2,1,0:T(8,128)} %param.7) | copy-start | bytes 1179652
  2.0 11.4 %collective-permute-start = (f32[8,6,1,8,128]{4,0,3,2,1:T(8,128)S(1)}, f32[8,6,1,8,128]{4,0,3,2,1:T(8,128)S(1)}, u32[]{:S(2)}, u32[]{:S(2)}) collective-permute-start(f32[8,6,1,8,128]{4,0,3,2,1:T(8,128)S(1)} %get-tuple-element.14), channel_id=1, source_target_pairs={{0,2},{2,4},{4,6},{6,8},{8,10},{10,12},{12,14},{14,0},{1,3},{3,5},... | collective-permute-start | bytes 589832 | tf_op jit(solution)/shard_map/ppermute | solution.py:19
  5.0 10.6 %collective-permute-start.1 = (f32[8,6,1,8,128]{4,0,3,2,1:T(8,128)S(1)}, f32[8,6,1,8,128]{4,0,3,2,1:T(8,128)S(1)}, u32[]{:S(2)}, u32[]{:S(2)}) collective-permute-start(f32[8,6,1,8,128]{4,0,3,2,1:T(8,128)S(1)} %get-tuple-element.15), channel_id=1, source_target_pairs={{2,0},{4,2},{6,4},{8,6},{10,8},{12,10},{14,12},{0,14},{3,1},{5,3},... | collective-permute-start | bytes 589832 | tf_op jit(solution)/shard_map/ppermute | solution.py:21
  10.8 6.1 %copy-start = (f32[8,6,6,2,8,128]{5,4,3,2,1,0:T(8,128)S(1)}, f32[8,6,6,2,8,128]{5,4,3,2,1,0:T(8,128)}, u32[]{:S(2)}) copy-start(f32[8,6,6,2,8,128]{5,4,3,2,1,0:T(8,128)} %param.8) | copy-start | bytes 7077892
  17.5 8.5 %collective-permute-start.2 = (f32[8,6,1,8,128]{4,0,3,2,1:T(8,128)S(1)}, f32[8,6,1,8,128]{4,0,3,2,1:T(8,128)S(1)}, u32[]{:S(2)}, u32[]{:S(2)}) collective-permute-start(f32[8,6,1,8,128]{4,0,3,2,1:T(8,128)S(1)} %get-tuple-element.6), channel_id=1, source_target_pairs={{0,2},{2,4},{4,6},{6,8},{8,10},{10,12},{12,14},{14,0},{1,3},{3,5},... | collective-permute-start | bytes 589832 | tf_op jit(solution)/shard_map/ppermute | solution.py:19
  17.9 11.5 %collective-permute-start.3 = (f32[8,6,1,8,128]{4,0,3,2,1:T(8,128)S(1)}, f32[8,6,1,8,128]{4,0,3,2,1:T(8,128)S(1)}, u32[]{:S(2)}, u32[]{:S(2)}) collective-permute-start(f32[8,6,1,8,128]{4,0,3,2,1:T(8,128)S(1)} %get-tuple-element.7), channel_id=1, source_target_pairs={{2,0},{4,2},{6,4},{8,6},{10,8},{12,10},{14,12},{0,14},{3,1},{5,3},... | collective-permute-start | bytes 589832 | tf_op jit(solution)/shard_map/ppermute | solution.py:21
  31.3 9.1 %collective-permute-start.4 = (f32[8,6,1,8,128]{4,0,3,2,1:T(8,128)S(1)}, f32[8,6,1,8,128]{4,0,3,2,1:T(8,128)S(1)}, u32[]{:S(2)}, u32[]{:S(2)}) collective-permute-start(f32[8,6,1,8,128]{4,0,3,2,1:T(8,128)S(1)} %get-tuple-element.4), channel_id=1, source_target_pairs={{0,2},{2,4},{4,6},{6,8},{8,10},{10,12},{12,14},{14,0},{1,3},{3,5},... | collective-permute-start | bytes 589832 | tf_op jit(solution)/shard_map/ppermute | solution.py:19
  31.4 11.9 %collective-permute-start.5 = (f32[8,6,1,8,128]{4,0,3,2,1:T(8,128)S(1)}, f32[8,6,1,8,128]{4,0,3,2,1:T(8,128)S(1)}, u32[]{:S(2)}, u32[]{:S(2)}) collective-permute-start(f32[8,6,1,8,128]{4,0,3,2,1:T(8,128)S(1)} %get-tuple-element.5), channel_id=1, source_target_pairs={{2,0},{4,2},{6,4},{8,6},{10,8},{12,10},{14,12},{0,14},{3,1},{5,3},... | collective-permute-start | bytes 589832 | tf_op jit(solution)/shard_map/ppermute | solution.py:21
  45.2 8.8 %collective-permute-start.6 = (f32[8,6,1,8,128]{4,0,3,2,1:T(8,128)S(1)}, f32[8,6,1,8,128]{4,0,3,2,1:T(8,128)S(1)}, u32[]{:S(2)}, u32[]{:S(2)}) collective-permute-start(f32[8,6,1,8,128]{4,0,3,2,1:T(8,128)S(1)} %get-tuple-element.2), channel_id=1, source_target_pairs={{0,2},{2,4},{4,6},{6,8},{8,10},{10,12},{12,14},{14,0},{1,3},{3,5},... | collective-permute-start | bytes 589832 | tf_op jit(solution)/shard_map/ppermute | solution.py:19
  45.3 11.9 %collective-permute-start.7 = (f32[8,6,1,8,128]{4,0,3,2,1:T(8,128)S(1)}, f32[8,6,1,8,128]{4,0,3,2,1:T(8,128)S(1)}, u32[]{:S(2)}, u32[]{:S(2)}) collective-permute-start(f32[8,6,1,8,128]{4,0,3,2,1:T(8,128)S(1)} %get-tuple-element.3), channel_id=1, source_target_pairs={{2,0},{4,2},{6,4},{8,6},{10,8},{12,10},{14,12},{0,14},{3,1},{5,3},... | collective-permute-start | bytes 589832 | tf_op jit(solution)/shard_map/ppermute | solution.py:21
  58.9 4.5 %copy-start.1 = (f32[8,2,8,128,6]{3,2,1,4,0:T(8,128)}, f32[8,2,8,128,6]{3,2,1,4,0:T(8,128)S(1)}, u32[]{:S(2)}) copy-start(f32[8,2,8,128,6]{3,2,1,4,0:T(8,128)S(1)} %multiply_reduce_fusion) | copy-start | bytes 1179652
  63.4 4.9 %copy-start.3 = (f32[8,3,6,256]{3,0,2,1:T(8,128)S(1)}, f32[8,3,6,256]{3,0,2,1:T(8,128)}, u32[]{:S(2)}) copy-start(f32[8,3,6,256]{3,0,2,1:T(8,128)} %param.11) | copy-start | bytes 442372
where the time goes:
time: 71.7 us; the launch traced here: 71.4 us
  starting transfers between devices  20.4 us (28%)
  waiting for transfers between devices  16.6 us (23%)
  local copies, waits for them, and re-layouts  12.6 us (18%)
  blocking collectives  12.6 us (18%)
  matrix products  5.1 us (7%)
  other arithmetic  3.09 us (4%)
  between operations  0.92 us (1%)
    ppermute x4, starting transfers between devices, extended(): lax.ppermute(head, axis, [((i + 1) % count, i) for i in range(count)])  17 us
    ppermute x4, waiting for transfers between devices, extended(): lax.ppermute(head, axis, [((i + 1) % count, i) for i in range(count)])  11.6 us
    all_gather x4, blocking collectives, body(): lax.all_gather(current, 'inst', axis=0, tiled=True)  9.57 us
    dot_general x4, matrix products, body(): jnp.einsum('mn,mvira->nvira', own_columns, lax.all_gather(current, 'inst'...  5.1 us
    ppermute x4, waiting for transfers between devices, extended(): lax.ppermute(tail, axis, [(i, (i + 1) % count) for i in range(count)])  5.03 us
    reshape x1, local copies, waits for them, and re-layouts, body(): flat_vector = adjoint.reshape(inst_dev, adjoint.shape[1], -1)  4.44 us
    gather x1, local copies, waits for them, and re-layouts, body(): selected_entries = jnp.take(flat_vector, surface_index, axis=2)  4.17 us
    ppermute x4, starting transfers between devices, extended(): lax.ppermute(tail, axis, [(i, (i + 1) % count) for i in range(count)])  3.44 us
  transfers between devices with their start and end apart: 8, of which 7 were waited for; matrix products, arithmetic and copies ran while one was open for 4% of the time, Pallas kernels for 0%

commit v1 on v0

v1 whole, which is shorter than its diff:
```python
import math

import jax
import jax.numpy as jnp
from jax import lax
from jax.experimental import pallas as pl
from jax.experimental.pallas import tpu as pltpu
from jax.sharding import PartitionSpec as P

SWEEPS = 4
SPECTRAL_WEIGHT = 0.25


def spectral_values(number):
    values = [0.0]
    for k in range(1, number):
        angle = math.pi * k / number
        values.append(SPECTRAL_WEIGHT * 0.5 * (-1) ** k * math.cos(angle) / math.sin(angle))
    return values


def update_layer(layer, own, partner, inner, halo, grad, diag, coupling, new, masked, resid):
    inst, variables, radial, axial = own.shape
    values = spectral_values(2 * inst)
    rows = lax.broadcasted_iota(jnp.int32, (radial, axial), 0)
    lanes = lax.broadcasted_iota(jnp.int32, (radial, axial), 1)
    edges = (rows > 0, rows < radial - 1, lanes > 0, lanes < axial - 1)
    for n in range(inst):
        for d, inside in enumerate(edges):
            masked[n, d] = jnp.where(inside, coupling[n, 2 + d, layer], 0.0)
    for u in range(variables):
        cycle = [own[m, u] for m in range(inst)] + [partner[m, u] for m in range(inst)]
        for n in range(inst):
            center = cycle[n]
            total = grad[n, u, layer]
            total = total + coupling[n, layer, layer] * halo[n, u]
            total = total + coupling[n, 1 - layer, layer] * inner[n, u]
            total = total + masked[n, 0] * pltpu.roll(center, 1, 0)
            total = total + masked[n, 1] * pltpu.roll(center, radial - 1, 0)
            total = total + masked[n, 2] * pltpu.roll(center, 1, 1)
            total = total + masked[n, 3] * pltpu.roll(center, axial - 1, 1)
            term = values[inst] * cycle[n + inst]
            for k in range(1, inst):
                term = term + values[k] * (cycle[(n + k) % (2 * inst)] - cycle[(n - k) % (2 * inst)])
            resid[n, u] = total - term
    for n in range(inst):
        terms = [resid[n, u] for u in range(variables)]
        for v in range(variables):
            total = diag[n, 0, v, layer] * terms[0]
            for u in range(1, variables):
                total = total + diag[n, u, v, layer] * terms[u]
            new[n, v] = total


def layer_sensitivity(layer, values, index, partials):
    inst, variables, radial, axial = values.shape
    surface = index.shape[1]
    place = index[...]
    lane = place % axial
    row = (place // axial) % radial
    select = lax.broadcasted_iota(jnp.int32, (axial, surface), 0) == jnp.broadcast_to(lane, (axial, surface))
    select = select.astype(jnp.float32).astype(jnp.bfloat16)
    here = (lax.broadcasted_iota(jnp.int32, (radial, surface), 0) == jnp.broadcast_to(row, (radial, surface))) & (
        jnp.broadcast_to(place // (axial * radial), (radial, surface)) == layer
    )
    flat = values[...].reshape(inst * variables * radial, axial)
    high = flat.astype(jnp.bfloat16)
    rest = flat - high.astype(jnp.float32)
    middle = rest.astype(jnp.bfloat16)
    low = (rest - middle.astype(jnp.float32)).astype(jnp.bfloat16)
    picked = jnp.dot(
        jnp.concatenate([high, middle, low], axis=1),
        jnp.concatenate([select, select, select], axis=0),
        preferred_element_type=jnp.float32,
    )
    sums = [jnp.zeros((radial, surface), jnp.float32) for _ in range(partials.shape[0])]
    for n in range(inst):
        for v in range(variables):
            start = (n * variables + v) * radial
            part = picked[start : start + radial]
            for k in range(len(sums)):
                sums[k] = sums[k] + part * jnp.broadcast_to(partials[k, v, n : n + 1, :], (radial, surface))
    return [jnp.sum(jnp.where(here, s, 0.0), axis=0, keepdims=True) for s in sums]


def sweep_kernel(layer_ref, own, partner, inner, halo, grad, diag, coupling, new, masked, resid):
    update_layer(layer_ref[0], own, partner, inner, halo, grad, diag, coupling, new, masked, resid)


def first_kernel(
    layer_ref, own, partner, inner, halo, grad, diag, coupling, index, partials, new, sens, masked, resid
):
    layer = layer_ref[0]
    update_layer(layer, own, partner, inner, halo, grad, diag, coupling, new, masked, resid)
    for k, row in enumerate(layer_sensitivity(layer, new, index, partials)):
        sens[k : k + 1, :] = row


def last_kernel(
    layer_ref,
    own,
    partner,
    inner,
    halo,
    grad,
    diag,
    coupling,
    index,
    partials,
    done,
    done_sens,
    adjoint,
    sens,
    new,
    masked,
    resid,
):
    layer = layer_ref[0]
    update_layer(layer, own, partner, inner, halo, grad, diag, coupling, new, masked, resid)
    for n in range(own.shape[0]):
        for v in range(own.shape[1]):
            adjoint[n, v, layer] = new[n, v]
            adjoint[n, v, 1 - layer] = done[n, v]
    for k, row in enumerate(layer_sensitivity(layer, new, index, partials)):
        sens[k : k + 1, :] = done_sens[k : k + 1, :] + row


def call(kernel, out_shapes, operands, scratch=()):
    inst, variables, radial, axial = operands[1].shape
    vmem = pl.BlockSpec(memory_space=pltpu.VMEM)
    return pl.pallas_call(
        kernel,
        out_shape=[jax.ShapeDtypeStruct(s, jnp.float32) for s in out_shapes],
        in_specs=[pl.BlockSpec(memory_space=pltpu.SMEM)] + [vmem] * (len(operands) - 1),
        out_specs=[vmem] * len(out_shapes),
        scratch_shapes=list(scratch)
        + [
            pltpu.VMEM((inst, 4, radial, axial), jnp.float32),
            pltpu.VMEM((inst, variables, radial, axial), jnp.float32),
        ],
        compiler_params=pltpu.CompilerParams(vmem_limit_bytes=24 * 1024 * 1024),
    )(*operands)


def body(
    adjoint_start, objective_grad, diag_inverse, face_coupling, surface_index, wall_point_partials
):
    count = lax.axis_size("blocks")
    assert count % 2 == 0 and lax.axis_size("inst") == 2 and adjoint_start.shape[2] == 2
    even_pairs = [(i, i ^ 1) for i in range(count)]
    odd_pairs = [(i, (((i + 1) ^ 1) - 1) % count) for i in range(count)]
    even_layer = 1 - lax.axis_index("blocks") % 2
    odd_layer = 1 - even_layer
    even_ref = even_layer.astype(jnp.int32).reshape(1)
    odd_ref = odd_layer.astype(jnp.int32).reshape(1)
    index = surface_index.reshape(1, -1)
    partials = jnp.transpose(wall_point_partials, (1, 2, 0, 3))

    def swap(layer, pairs):
        return lax.ppermute(layer, "blocks", pairs)

    def cores(layer):
        return lax.ppermute(layer, "inst", [(0, 1), (1, 0)])

    even = lax.dynamic_index_in_dim(adjoint_start, even_layer, 2, keepdims=False)
    odd = lax.dynamic_index_in_dim(adjoint_start, odd_layer, 2, keepdims=False)
    shape = even.shape
    fixed = (objective_grad, diag_inverse, face_coupling)
    for sweep in range(SWEEPS):
        even_halo = swap(even, even_pairs)
        odd_halo = swap(odd, odd_pairs)
        even_partner = cores(even)
        odd_partner = cores(odd)
        even_args = (even_ref, even, even_partner, odd, even_halo, *fixed)
        odd_args = (odd_ref, odd, odd_partner, even, odd_halo, *fixed)
        if sweep < SWEEPS - 1:
            (even,) = call(sweep_kernel, [shape], even_args)
            (odd,) = call(sweep_kernel, [shape], odd_args)
    sens_shape = (partials.shape[0], surface_index.shape[0])
    even, sens = call(first_kernel, [shape, sens_shape], (*even_args, index, partials))
    adjoint, sens = call(
        last_kernel,
        [adjoint_start.shape, sens_shape],
        (*odd_args, index, partials, even, sens),
        [pltpu.VMEM(shape, jnp.float32)],
    )
    return adjoint, sens + cores(sens)


def solution(mesh):
    return jax.shard_map(
        body,
        mesh=mesh,
        in_specs=(
            P(("groups", "inst"), None, "blocks", None, None),
            P(("groups", "inst"), None, "blocks", None, None),
            P(("groups", "inst"), None, None, "blocks", None, None),
            P(("groups", "inst"), None, "blocks", None, None),
            P(("groups", "blocks")),
            P(("groups", "inst"), None, None, "blocks"),
        ),
        out_specs=(
            P(("groups", "inst"), None, "blocks", None, None),
            P(None, ("groups", "blocks")),
        ),
        check_vma=False,
    )
```

time: 71.7 us -> 58.1 us (0.81)
  blocking collectives: 12.6 us -> 0 us
  local copies, waits for them, and re-layouts: 12.6 us -> 4.79 us
  starting transfers between devices: 20.4 us -> 26.7 us
  matrix products: 5.1 us -> 0 us
  waiting for transfers between devices: 16.6 us -> 21 us
  Pallas kernels: 0 us -> 4 us
  other arithmetic: 3.09 us -> 0.6 us
    all_gather x4 -> x0, blocking collectives: 9.57 us -> none  [body(): lax.all_gather(current, 'inst', axis=0, tiled=True)]
    ppermute x8 -> x17, starting transfers between devices: 20.4 us -> 26.7 us  [the longest x8 25.1 us: swap(): return lax.ppermute(layer, 'blocks', pairs)]
    dot_general x4 -> x0, matrix products: 5.1 us -> none  [body(): jnp.einsum('mn,mvira->nvira', own_columns, lax.all_gather(current, 'inst'...]
    reshape x1 -> x0, local copies, waits for them, and re-layouts: 4.44 us -> none  [body(): flat_vector = adjoint.reshape(inst_dev, adjoint.shape[1], -1)]
    ppermute x8 -> x17, waiting for transfers between devices: 16.6 us -> 21 us  [the longest x8 19.8 us: swap(): return lax.ppermute(layer, 'blocks', pairs)]
    gather x1 -> x0, local copies, waits for them, and re-layouts: 4.17 us -> none  [body(): selected_entries = jnp.take(flat_vector, surface_index, axis=2)]
    pallas_call x0 -> x8, Pallas kernels: none -> 4 us  [call(): pl.pallas_call(kernel, out_shape=[jax.ShapeDtypeStruct(s, jnp.float32) fo...]
    psum x1 -> x0, blocking collectives: 3.06 us -> none  [body(): sensitivity = lax.psum(local_terms, 'inst')]
  transfers between devices with their start and end apart: 8 -> 17, of which waited for: 7 -> 6; matrix products, arithmetic and copies ran while one was open for 4% -> 0% of each run, Pallas kernels for 0% -> 5%
where the time goes in v1:
time: 58.1 us; the launch traced here: 57.9 us
  starting transfers between devices  26.7 us (46%)
  waiting for transfers between devices  21 us (36%)
  local copies, waits for them, and re-layouts  4.79 us (8%)
  Pallas kernels  4 us (7%)
  between operations  0.77 us (1%)
  other arithmetic  0.6 us (1%)
    ppermute x8, starting transfers between devices, swap(): return lax.ppermute(layer, 'blocks', pairs)  25.1 us
    ppermute x8, waiting for transfers between devices, swap(): return lax.ppermute(layer, 'blocks', pairs)  19.8 us
    pallas_call x8, Pallas kernels, call(): pl.pallas_call(kernel, out_shape=[jax.ShapeDtypeStruct(s, jnp.float32) fo...  4 us
    unnamed x16, local copies, waits for them, and re-layouts  3.68 us
    ppermute x9, starting transfers between devices, cores(): return lax.ppermute(layer, 'inst', [(0, 1), (1, 0)])  1.59 us
    ppermute x9, waiting for transfers between devices, cores(): return lax.ppermute(layer, 'inst', [(0, 1), (1, 0)])  1.18 us
  transfers between devices with their start and end apart: 17, of which 6 were waited for; matrix products, arithmetic and copies ran while one was open for 0% of the time, Pallas kernels for 5%

profile of v1, /device:TPU:0, one launch (start us, length us, event | category | flops | bytes accessed | tf_op | source)
XLA Modules:
  0.0 57.9 jit_solution(12913752534394669461)
XLA Ops:
  0.7 0.0 copy-start.3
  0.7 1.1 %dynamic-slice_bitcast_fusion = (f32[8,6,8,128]{3,2,1,0:T(8,128)S(1)}, f32[8,6,8,128]{3,2,1,0:T(8,128)S(1)}) fusion(f32[8,6,2,8,128]{4,3,2,1,0:T(8,128)} %param.6, s32[]{:T(128)S(6)} %select_n.16, s32[]{:T(128)S(6)} %select_n.15), kind=kLoop, calls=%fused_computation | loop fusion | bytes 786440 | tf_op jit(solution)/shard_map/jit(dynamic_index_in_dim)/squeeze | solution.py:165
  1.8 0.5 collective-permute-start.3
  2.3 2.6 %collective-permute-start.4 = (f32[8,6,8,128]{3,2,1,0:T(8,128)S(1)}, f32[8,6,8,128]{3,2,1,0:T(8,128)S(1)}, u32[]{:S(2)}, u32[]{:S(2)}) collective-permute-start(f32[8,6,8,128]{3,2,1,0:T(8,128)S(1)} %get-tuple-element.10.inner.own), channel_id=1, source_target_pairs={{0,2},{2,0},{4,6},{6,4},{8,10},{10,8},{12,14},{14,12},{1,3},{3,1},... | collective-permute-start | bytes 589832 | tf_op jit(solution)/shard_map/ppermute | solution.py:160
  4.9 0.2 collective-permute-start
  5.0 3.6 %collective-permute-start.1 = (f32[8,6,8,128]{3,2,1,0:T(8,128)S(1)}, f32[8,6,8,128]{3,2,1,0:T(8,128)S(1)}, u32[]{:S(2)}, u32[]{:S(2)}) collective-permute-start(f32[8,6,8,128]{3,2,1,0:T(8,128)S(1)} %get-tuple-element.11.own.inner), channel_id=1, source_target_pairs={{0,14},{2,4},{4,2},{6,8},{8,6},{10,12},{12,10},{14,0},{1,15},{3,5}... | collective-permute-start | bytes 589832 | tf_op jit(solution)/shard_map/ppermute | solution.py:160
  8.6 0.0 collective-permute-done.3.partner
  8.6 5.2 %collective-permute-done.4.halo = f32[8,6,8,128]{3,2,1,0:T(8,128)S(1)} collective-permute-done((f32[8,6,8,128]{3,2,1,0:T(8,128)S(1)}, f32[8,6,8,128]{3,2,1,0:T(8,128)S(1)}, u32[]{:S(2)}, u32[]{:S(2)}) %collective-permute-start.4) | collective-permute-done | bytes 196640 | tf_op jit(solution)/shard_map/ppermute | solution.py:160
  13.8 0.0 copy-start
  13.8 1.7 %copy-done = f32[8,6,6,2,8,128]{5,4,3,2,1,0:T(8,128)S(1)} copy-done((f32[8,6,6,2,8,128]{5,4,3,2,1,0:T(8,128)S(1)}, f32[8,6,6,2,8,128]{5,4,3,2,1,0:T(8,128)}, u32[]{:S(2)}) %copy-start) | copy-done | bytes 2359320
  15.5 0.0 copy-start.2
  15.5 1.0 %copy-done.2 = f32[8,6,2,8,128]{4,3,2,1,0:T(8,128)S(1)} copy-done((f32[8,6,2,8,128]{4,3,2,1,0:T(8,128)S(1)}, f32[8,6,2,8,128]{4,3,2,1,0:T(8,128)}, u32[]{:S(2)}) %copy-start.2) | copy-done | bytes 393240
  16.5 0.0 copy-start.4
  16.5 1.0 %copy-done.4 = f32[8,6,2,8,128]{4,3,2,1,0:T(8,128)S(1)} copy-done((f32[8,6,2,8,128]{4,3,2,1,0:T(8,128)S(1)}, f32[8,6,2,8,128]{4,3,2,1,0:T(8,128)}, u32[]{:S(2)}) %copy-start.4) | copy-done | bytes 393240
  17.5 0.0 copy-start.1
  17.5 0.4 shard_map.78.inner.own
  17.9 0.0 copy-start.5
  17.9 0.1 collective-permute-start.7
  18.0 2.5 %collective-permute-start.8 = (f32[8,6,8,128]{3,2,1,0:T(8,128)S(1)}, f32[8,6,8,128]{3,2,1,0:T(8,128)S(1)}, u32[]{:S(2)}, u32[]{:S(2)}) collective-permute-start(f32[8,6,8,128]{3,2,1,0:T(8,128)S(1)} %shard_map.78.inner.own), channel_id=1, source_target_pairs={{0,2},{2,0},{4,6},{6,4},{8,10},{10,8},{12,14},{14,12},{1,3},{3,1},... | collective-permute-start | bytes 589832 | tf_op jit(solution)/shard_map/ppermute | solution.py:160
  20.5 0.0 collective-permute-done.partner
  20.5 0.0 collective-permute-done.1.halo
  20.5 0.0 copy-done.3
  20.5 0.0 copy-done.1
  20.5 0.4 shard_map.77.own.inner
  20.9 0.2 collective-permute-start.2
  21.1 4.1 %collective-permute-start.5 = (f32[8,6,8,128]{3,2,1,0:T(8,128)S(1)}, f32[8,6,8,128]{3,2,1,0:T(8,128)S(1)}, u32[]{:S(2)}, u32[]{:S(2)}) collective-permute-start(f32[8,6,8,128]{3,2,1,0:T(8,128)S(1)} %shard_map.77.own.inner), channel_id=1, source_target_pairs={{0,14},{2,4},{4,2},{6,8},{8,6},{10,12},{12,10},{14,0},{1,15},{3,5}... | collective-permute-start | bytes 589832 | tf_op jit(solution)/shard_map/ppermute | solution.py:160
  25.2 0.0 collective-permute-done.7.partner
  25.2 4.3 %collective-permute-done.8.halo = f32[8,6,8,128]{3,2,1,0:T(8,128)S(1)} collective-permute-done((f32[8,6,8,128]{3,2,1,0:T(8,128)S(1)}, f32[8,6,8,128]{3,2,1,0:T(8,128)S(1)}, u32[]{:S(2)}, u32[]{:S(2)}) %collective-permute-start.8) | collective-permute-done | bytes 196640 | tf_op jit(solution)/shard_map/ppermute | solution.py:160
  29.5 0.0 copy-done.5
  29.5 0.4 shard_map.80.inner.own
  29.9 0.1 collective-permute-start.11
  30.0 2.5 %collective-permute-start.12 = (f32[8,6,8,128]{3,2,1,0:T(8,128)S(1)}, f32[8,6,8,128]{3,2,1,0:T(8,128)S(1)}, u32[]{:S(2)}, u32[]{:S(2)}) collective-permute-start(f32[8,6,8,128]{3,2,1,0:T(8,128)S(1)} %shard_map.80.inner.own), channel_id=1, source_target_pairs={{0,2},{2,0},{4,6},{6,4},{8,10},{10,8},{12,14},{14,12},{1,3},{3,1},... | collective-permute-start | bytes 589832 | tf_op jit(solution)/shard_map/ppermute | solution.py:160
  32.5 0.0 collective-permute-done.2.partner
  32.5 0.0 collective-permute-done.5.halo
  32.5 0.4 shard_map.79.own.inner
  32.9 0.2 collective-permute-start.6
  33.1 3.6 %collective-permute-start.9 = (f32[8,6,8,128]{3,2,1,0:T(8,128)S(1)}, f32[8,6,8,128]{3,2,1,0:T(8,128)S(1)}, u32[]{:S(2)}, u32[]{:S(2)}) collective-permute-start(f32[8,6,8,128]{3,2,1,0:T(8,128)S(1)} %shard_map.79.own.inner), channel_id=1, source_target_pairs={{0,14},{2,4},{4,2},{6,8},{8,6},{10,12},{12,10},{14,0},{1,15},{3,5}... | collective-permute-start | bytes 589832 | tf_op jit(solution)/shard_map/ppermute | solution.py:160
  36.7 0.0 collective-permute-done.11.partner
  36.7 4.7 %collective-permute-done.12.halo = f32[8,6,8,128]{3,2,1,0:T(8,128)S(1)} collective-permute-done((f32[8,6,8,128]{3,2,1,0:T(8,128)S(1)}, f32[8,6,8,128]{3,2,1,0:T(8,128)S(1)}, u32[]{:S(2)}, u32[]{:S(2)}) %collective-permute-start.12) | collective-permute-done | bytes 196640 | tf_op jit(solution)/shard_map/ppermute | solution.py:160
  41.5 0.4 shard_map.82.own.inner
  41.9 0.0 copy-start.6
  41.9 0.0 copy-start.7
  41.9 0.1 collective-permute-start.14
  42.0 2.5 %collective-permute-start.15 = (f32[8,6,8,128]{3,2,1,0:T(8,128)S(1)}, f32[8,6,8,128]{3,2,1,0:T(8,128)S(1)}, u32[]{:S(2)}, u32[]{:S(2)}) collective-permute-start(f32[8,6,8,128]{3,2,1,0:T(8,128)S(1)} %shard_map.82.own.inner), channel_id=1, source_target_pairs={{0,2},{2,0},{4,6},{6,4},{8,10},{10,8},{12,14},{14,12},{1,3},{3,1},... | collective-permute-start | bytes 589832 | tf_op jit(solution)/shard_map/ppermute | solution.py:160
  44.5 0.0 collective-permute-done.6.partner
  44.5 0.0 collective-permute-done.9.halo
  44.5 0.4 shard_map.81.inner.own
  44.9 0.2 collective-permute-start.10
  45.1 3.7 %collective-permute-start.13 = (f32[8,6,8,128]{3,2,1,0:T(8,128)S(1)}, f32[8,6,8,128]{3,2,1,0:T(8,128)S(1)}, u32[]{:S(2)}, u32[]{:S(2)}) collective-permute-start(f32[8,6,8,128]{3,2,1,0:T(8,128)S(1)} %shard_map.81.inner.own), channel_id=1, source_target_pairs={{0,14},{2,4},{4,2},{6,8},{8,6},{10,12},{12,10},{14,0},{1,15},{3,5}... | collective-permute-start | bytes 589832 | tf_op jit(solution)/shard_map/ppermute | solution.py:160
  48.7 0.0 collective-permute-done.14.partner
  48.8 4.7 %collective-permute-done.15.halo = f32[8,6,8,128]{3,2,1,0:T(8,128)S(1)} collective-permute-done((f32[8,6,8,128]{3,2,1,0:T(8,128)S(1)}, f32[8,6,8,128]{3,2,1,0:T(8,128)S(1)}, u32[]{:S(2)}, u32[]{:S(2)}) %collective-permute-start.15) | collective-permute-done | bytes 196640 | tf_op jit(solution)/shard_map/ppermute | solution.py:160
  53.5 0.0 copy-done.6
  53.5 0.0 copy-done.7
  53.5 0.6 %shard_map.83 = (f32[8,6,8,128]{3,2,1,0:T(8,128)S(1)}, f32[3,256]{1,0:T(4,128)S(1)}) custom-call(s32[1]{0:T(128)} %bitcast.3.layer_ref, f32[8,6,8,128]{3,2,1,0:T(8,128)S(1)} %shard_map.82.own.inner, f32[8,6,8,128]{3,2,1,0:T(8,128)S(1)} %collective-permute-done.14.partner, f32[8,6,8,128]{3,2,1,0:T(8,128)S(1)} %shard_map.81.inner.own, ...), custom_call_target="tpu_custom_call" | custom-call | tf_op jit(solution)/shard_map/pallas_call | solution.py:131
  54.1 0.0 collective-permute-done.10.partner
  54.1 0.9 %collective-permute-done.13.halo = f32[8,6,8,128]{3,2,1,0:T(8,128)S(1)} collective-permute-done((f32[8,6,8,128]{3,2,1,0:T(8,128)S(1)}, f32[8,6,8,128]{3,2,1,0:T(8,128)S(1)}, u32[]{:S(2)}, u32[]{:S(2)}) %collective-permute-start.13) | collective-permute-done | bytes 196640 | tf_op jit(solution)/shard_map/ppermute | solution.py:160
  54.9 1.2 %shard_map.84 = (f32[8,6,2,8,128]{4,3,2,1,0:T(8,128)}, f32[3,256]{1,0:T(4,128)S(1)}) custom-call(s32[1]{0:T(128)} %bitcast.layer_ref, f32[8,6,8,128]{3,2,1,0:T(8,128)S(1)} %shard_map.81.inner.own, f32[8,6,8,128]{3,2,1,0:T(8,128)S(1)} %collective-permute-done.10.partner, f32[8,6,8,128]{3,2,1,0:T(8,128)S(1)} %shard_map.82.own.inner, ...), custom_call_target="tpu_custom_call" | custom-call | tf_op jit(solution)/shard_map/pallas_call | solution.py:131
  56.1 0.0 collective-permute-start.16
  56.1 1.2 %collective-permute-done.16 = f32[3,256]{1,0:T(4,128)S(1)} collective-permute-done((f32[3,256]{1,0:T(4,128)S(1)}, f32[3,256]{1,0:T(4,128)S(1)}, u32[]{:S(2)}, u32[]{:S(2)}) %collective-permute-start.16) | collective-permute-done | bytes 3104 | tf_op jit(solution)/shard_map/ppermute | solution.py:163
  57.3 0.6 %add.18 = f32[3,256]{1,0:T(4,128)} add(f32[3,256]{1,0:T(4,128)S(1)} %get-tuple-element.9, f32[3,256]{1,0:T(4,128)S(1)} %collective-permute-done.16) | non-fusion elementwise | flops 768 | bytes 9216 | tf_op jit(solution)/shard_map/add | solution.py:187
Async XLA Ops:
  0.7 19.9 %copy-start.3 = (f32[8,6,2,8,128]{4,3,2,1,0:T(8,128)S(1)}, f32[8,6,2,8,128]{4,3,2,1,0:T(8,128)}, u32[]{:S(2)}) copy-start(f32[8,6,2,8,128]{4,3,2,1,0:T(8,128)} %grad.15) | copy-start | bytes 1179652
  1.8 6.8 %collective-permute-start.3 = (f32[8,6,8,128]{3,2,1,0:T(8,128)S(1)}, f32[8,6,8,128]{3,2,1,0:T(8,128)S(1)}, u32[]{:S(2)}, u32[]{:S(2)}) collective-permute-start(f32[8,6,8,128]{3,2,1,0:T(8,128)S(1)} %get-tuple-element.10.inner.own), channel_id=1, source_target_pairs={{0,1},{1,0},{2,3},{3,2},{4,5},{5,4},{6,7},{7,6},{8,9},{9,8},{10,11... | collective-permute-start | bytes 589832 | tf_op jit(solution)/shard_map/ppermute | solution.py:163
  2.3 11.5 %collective-permute-start.4 = (f32[8,6,8,128]{3,2,1,0:T(8,128)S(1)}, f32[8,6,8,128]{3,2,1,0:T(8,128)S(1)}, u32[]{:S(2)}, u32[]{:S(2)}) collective-permute-start(f32[8,6,8,128]{3,2,1,0:T(8,128)S(1)} %get-tuple-element.10.inner.own), channel_id=1, source_target_pairs={{0,2},{2,0},{4,6},{6,4},{8,10},{10,8},{12,14},{14,12},{1,3},{3,1},... | collective-permute-start | bytes 589832 | tf_op jit(solution)/shard_map/ppermute | solution.py:160
  4.9 15.7 %collective-permute-start = (f32[8,6,8,128]{3,2,1,0:T(8,128)S(1)}, f32[8,6,8,128]{3,2,1,0:T(8,128)S(1)}, u32[]{:S(2)}, u32[]{:S(2)}) collective-permute-start(f32[8,6,8,128]{3,2,1,0:T(8,128)S(1)} %get-tuple-element.11.own.inner), channel_id=1, source_target_pairs={{0,1},{1,0},{2,3},{3,2},{4,5},{5,4},{6,7},{7,6},{8,9},{9,8},{10,11... | collective-permute-start | bytes 589832 | tf_op jit(solution)/shard_map/ppermute | solution.py:163
  5.0 15.5 %collective-permute-start.1 = (f32[8,6,8,128]{3,2,1,0:T(8,128)S(1)}, f32[8,6,8,128]{3,2,1,0:T(8,128)S(1)}, u32[]{:S(2)}, u32[]{:S(2)}) collective-permute-start(f32[8,6,8,128]{3,2,1,0:T(8,128)S(1)} %get-tuple-element.11.own.inner), channel_id=1, source_target_pairs={{0,14},{2,4},{4,2},{6,8},{8,6},{10,12},{12,10},{14,0},{1,15},{3,5}... | collective-permute-start | bytes 589832 | tf_op jit(solution)/shard_map/ppermute | solution.py:160
  13.8 1.7 %copy-start = (f32[8,6,6,2,8,128]{5,4,3,2,1,0:T(8,128)S(1)}, f32[8,6,6,2,8,128]{5,4,3,2,1,0:T(8,128)}, u32[]{:S(2)}) copy-start(f32[8,6,6,2,8,128]{5,4,3,2,1,0:T(8,128)} %diag.15) | copy-start | bytes 7077892
  15.5 1.0 %copy-start.2 = (f32[8,6,2,8,128]{4,3,2,1,0:T(8,128)S(1)}, f32[8,6,2,8,128]{4,3,2,1,0:T(8,128)}, u32[]{:S(2)}) copy-start(f32[8,6,2,8,128]{4,3,2,1,0:T(8,128)} %grad.15) | copy-start | bytes 1179652
  16.5 1.0 %copy-start.4 = (f32[8,6,2,8,128]{4,3,2,1,0:T(8,128)S(1)}, f32[8,6,2,8,128]{4,3,2,1,0:T(8,128)}, u32[]{:S(2)}) copy-start(f32[8,6,2,8,128]{4,3,2,1,0:T(8,128)} %coupling.15) | copy-start | bytes 1179652
  17.5 3.0 %copy-start.1 = (f32[8,6,6,2,8,128]{5,4,3,2,1,0:T(8,128)S(1)}, f32[8,6,6,2,8,128]{5,4,3,2,1,0:T(8,128)}, u32[]{:S(2)}) copy-start(f32[8,6,6,2,8,128]{5,4,3,2,1,0:T(8,128)} %diag.15) | copy-start | bytes 7077892
  17.9 11.6 %copy-start.5 = (f32[8,6,2,8,128]{4,3,2,1,0:T(8,128)S(1)}, f32[8,6,2,8,128]{4,3,2,1,0:T(8,128)}, u32[]{:S(2)}) copy-start(f32[8,6,2,8,128]{4,3,2,1,0:T(8,128)} %coupling.15) | copy-start | bytes 1179652
  17.9 7.3 %collective-permute-start.7 = (f32[8,6,8,128]{3,2,1,0:T(8,128)S(1)}, f32[8,6,8,128]{3,2,1,0:T(8,128)S(1)}, u32[]{:S(2)}, u32[]{:S(2)}) collective-permute-start(f32[8,6,8,128]{3,2,1,0:T(8,128)S(1)} %shard_map.78.inner.own), channel_id=1, source_target_pairs={{0,1},{1,0},{2,3},{3,2},{4,5},{5,4},{6,7},{7,6},{8,9},{9,8},{10,11... | collective-permute-start | bytes 589832 | tf_op jit(solution)/shard_map/ppermute | solution.py:163
  18.0 11.5 %collective-permute-start.8 = (f32[8,6,8,128]{3,2,1,0:T(8,128)S(1)}, f32[8,6,8,128]{3,2,1,0:T(8,128)S(1)}, u32[]{:S(2)}, u32[]{:S(2)}) collective-permute-start(f32[8,6,8,128]{3,2,1,0:T(8,128)S(1)} %shard_map.78.inner.own), channel_id=1, source_target_pairs={{0,2},{2,0},{4,6},{6,4},{8,10},{10,8},{12,14},{14,12},{1,3},{3,1},... | collective-permute-start | bytes 589832 | tf_op jit(solution)/shard_map/ppermute | solution.py:160
  20.9 11.6 %collective-permute-start.2 = (f32[8,6,8,128]{3,2,1,0:T(8,128)S(1)}, f32[8,6,8,128]{3,2,1,0:T(8,128)S(1)}, u32[]{:S(2)}, u32[]{:S(2)}) collective-permute-start(f32[8,6,8,128]{3,2,1,0:T(8,128)S(1)} %shard_map.77.own.inner), channel_id=1, source_target_pairs={{0,1},{1,0},{2,3},{3,2},{4,5},{5,4},{6,7},{7,6},{8,9},{9,8},{10,11... | collective-permute-start | bytes 589832 | tf_op jit(solution)/shard_map/ppermute | solution.py:163
  21.1 11.4 %collective-permute-start.5 = (f32[8,6,8,128]{3,2,1,0:T(8,128)S(1)}, f32[8,6,8,128]{3,2,1,0:T(8,128)S(1)}, u32[]{:S(2)}, u32[]{:S(2)}) collective-permute-start(f32[8,6,8,128]{3,2,1,0:T(8,128)S(1)} %shard_map.77.own.inner), channel_id=1, source_target_pairs={{0,14},{2,4},{4,2},{6,8},{8,6},{10,12},{12,10},{14,0},{1,15},{3,5}... | collective-permute-start | bytes 589832 | tf_op jit(solution)/shard_map/ppermute | solution.py:160
  29.9 6.8 %collective-permute-start.11 = (f32[8,6,8,128]{3,2,1,0:T(8,128)S(1)}, f32[8,6,8,128]{3,2,1,0:T(8,128)S(1)}, u32[]{:S(2)}, u32[]{:S(2)}) collective-permute-start(f32[8,6,8,128]{3,2,1,0:T(8,128)S(1)} %shard_map.80.inner.own), channel_id=1, source_target_pairs={{0,1},{1,0},{2,3},{3,2},{4,5},{5,4},{6,7},{7,6},{8,9},{9,8},{10,11... | collective-permute-start | bytes 589832 | tf_op jit(solution)/shard_map/ppermute | solution.py:163
  30.0 11.5 %collective-permute-start.12 = (f32[8,6,8,128]{3,2,1,0:T(8,128)S(1)}, f32[8,6,8,128]{3,2,1,0:T(8,128)S(1)}, u32[]{:S(2)}, u32[]{:S(2)}) collective-permute-start(f32[8,6,8,128]{3,2,1,0:T(8,128)S(1)} %shard_map.80.inner.own), channel_id=1, source_target_pairs={{0,2},{2,0},{4,6},{6,4},{8,10},{10,8},{12,14},{14,12},{1,3},{3,1},... | collective-permute-start | bytes 589832 | tf_op jit(solution)/shard_map/ppermute | solution.py:160
  32.9 11.6 %collective-permute-start.6 = (f32[8,6,8,128]{3,2,1,0:T(8,128)S(1)}, f32[8,6,8,128]{3,2,1,0:T(8,128)S(1)}, u32[]{:S(2)}, u32[]{:S(2)}) collective-permute-start(f32[8,6,8,128]{3,2,1,0:T(8,128)S(1)} %shard_map.79.own.inner), channel_id=1, source_target_pairs={{0,1},{1,0},{2,3},{3,2},{4,5},{5,4},{6,7},{7,6},{8,9},{9,8},{10,11... | collective-permute-start | bytes 589832 | tf_op jit(solution)/shard_map/ppermute | solution.py:163
  33.1 11.4 %collective-permute-start.9 = (f32[8,6,8,128]{3,2,1,0:T(8,128)S(1)}, f32[8,6,8,128]{3,2,1,0:T(8,128)S(1)}, u32[]{:S(2)}, u32[]{:S(2)}) collective-permute-start(f32[8,6,8,128]{3,2,1,0:T(8,128)S(1)} %shard_map.79.own.inner), channel_id=1, source_target_pairs={{0,14},{2,4},{4,2},{6,8},{8,6},{10,12},{12,10},{14,0},{1,15},{3,5}... | collective-permute-start | bytes 589832 | tf_op jit(solution)/shard_map/ppermute | solution.py:160
  41.9 11.6 %copy-start.6 = (f32[8,3,6,256]{3,0,2,1:T(8,128)S(1)}, f32[8,3,6,256]{3,0,2,1:T(8,128)}, u32[]{:S(2)}) copy-start(f32[8,3,6,256]{3,0,2,1:T(8,128)} %param.11) | copy-start | bytes 442372
  41.9 11.6 %copy-start.7 = (s32[256]{0:T(256)S(1)}, s32[256]{0:T(256)}, u32[]{:S(2)}) copy-start(s32[256]{0:T(256)} %param.10) | copy-start | bytes 3076
  41.9 6.9 %collective-permute-start.14 = (f32[8,6,8,128]{3,2,1,0:T(8,128)S(1)}, f32[8,6,8,128]{3,2,1,0:T(8,128)S(1)}, u32[]{:S(2)}, u32[]{:S(2)}) collective-permute-start(f32[8,6,8,128]{3,2,1,0:T(8,128)S(1)} %shard_map.82.own.inner), channel_id=1, source_target_pairs={{0,1},{1,0},{2,3},{3,2},{4,5},{5,4},{6,7},{7,6},{8,9},{9,8},{10,11... | collective-permute-start | bytes 589832 | tf_op jit(solution)/shard_map/ppermute | solution.py:163
  42.0 11.5 %collective-permute-start.15 = (f32[8,6,8,128]{3,2,1,0:T(8,128)S(1)}, f32[8,6,8,128]{3,2,1,0:T(8,128)S(1)}, u32[]{:S(2)}, u32[]{:S(2)}) collective-permute-start(f32[8,6,8,128]{3,2,1,0:T(8,128)S(1)} %shard_map.82.own.inner), channel_id=1, source_target_pairs={{0,2},{2,0},{4,6},{6,4},{8,10},{10,8},{12,14},{14,12},{1,3},{3,1},... | collective-permute-start | bytes 589832 | tf_op jit(solution)/shard_map/ppermute | solution.py:160
  44.9 9.2 %collective-permute-start.10 = (f32[8,6,8,128]{3,2,1,0:T(8,128)S(1)}, f32[8,6,8,128]{3,2,1,0:T(8,128)S(1)}, u32[]{:S(2)}, u32[]{:S(2)}) collective-permute-start(f32[8,6,8,128]{3,2,1,0:T(8,128)S(1)} %shard_map.81.inner.own), channel_id=1, source_target_pairs={{0,1},{1,0},{2,3},{3,2},{4,5},{5,4},{6,7},{7,6},{8,9},{9,8},{10,11... | collective-permute-start | bytes 589832 | tf_op jit(solution)/shard_map/ppermute | solution.py:163
  45.1 9.8 %collective-permute-start.13 = (f32[8,6,8,128]{3,2,1,0:T(8,128)S(1)}, f32[8,6,8,128]{3,2,1,0:T(8,128)S(1)}, u32[]{:S(2)}, u32[]{:S(2)}) collective-permute-start(f32[8,6,8,128]{3,2,1,0:T(8,128)S(1)} %shard_map.81.inner.own), channel_id=1, source_target_pairs={{0,14},{2,4},{4,2},{6,8},{8,6},{10,12},{12,10},{14,0},{1,15},{3,5}... | collective-permute-start | bytes 589832 | tf_op jit(solution)/shard_map/ppermute | solution.py:160
  56.1 1.2 %collective-permute-start.16 = (f32[3,256]{1,0:T(4,128)S(1)}, f32[3,256]{1,0:T(4,128)S(1)}, u32[]{:S(2)}, u32[]{:S(2)}) collective-permute-start(f32[3,256]{1,0:T(4,128)S(1)} %get-tuple-element.9), channel_id=1, source_target_pairs={{0,1},{1,0},{2,3},{3,2},{4,5},{5,4},{6,7},{7,6},{8,9},{9,8},{10,11... | collective-permute-start | bytes 9224 | tf_op jit(solution)/shard_map/ppermute | solution.py:163

commit v2 on v1

v2 whole, which is shorter than its diff:
```python
import math

import jax
import jax.numpy as jnp
from jax import lax
from jax.experimental import pallas as pl
from jax.experimental.pallas import tpu as pltpu
from jax.sharding import PartitionSpec as P

SWEEPS = 4
CHUNKS = (1, 1)
SPECTRAL_WEIGHT = 0.25


def spectral_values(number):
    values = [0.0]
    for k in range(1, number):
        angle = math.pi * k / number
        values.append(SPECTRAL_WEIGHT * 0.5 * (-1) ** k * math.cos(angle) / math.sin(angle))
    return values


def update_chunk(layer, start, own, partner, inner, halo, grad, diag, coupling, new, masked, resid):
    inst, variables, radial, axial = own.shape
    size = new.shape[0]
    skip = start if halo.shape[0] == inst else 0
    values = spectral_values(2 * inst)
    rows = lax.broadcasted_iota(jnp.int32, (radial, axial), 0)
    lanes = lax.broadcasted_iota(jnp.int32, (radial, axial), 1)
    edges = (rows > 0, rows < radial - 1, lanes > 0, lanes < axial - 1)
    for i in range(size):
        for d, inside in enumerate(edges):
            masked[i, d] = jnp.where(inside, coupling[start + i, 2 + d, layer], 0.0)
    for u in range(variables):
        cycle = [own[m, u] for m in range(inst)] + [partner[m, u] for m in range(inst)]
        for i in range(size):
            n = start + i
            center = cycle[n]
            total = grad[n, u, layer]
            total = total + coupling[n, layer, layer] * halo[skip + i, u]
            total = total + coupling[n, 1 - layer, layer] * inner[n, u]
            total = total + masked[i, 0] * pltpu.roll(center, 1, 0)
            total = total + masked[i, 1] * pltpu.roll(center, radial - 1, 0)
            total = total + masked[i, 2] * pltpu.roll(center, 1, 1)
            total = total + masked[i, 3] * pltpu.roll(center, axial - 1, 1)
            term = values[inst] * cycle[(n + inst) % (2 * inst)]
            for k in range(1, inst):
                term = term + values[k] * (cycle[(n + k) % (2 * inst)] - cycle[(n - k) % (2 * inst)])
            resid[i, u] = total - term
    for i in range(size):
        terms = [resid[i, u] for u in range(variables)]
        for v in range(variables):
            total = diag[start + i, 0, v, layer] * terms[0]
            for u in range(1, variables):
                total = total + diag[start + i, u, v, layer] * terms[u]
            new[i, v] = total


def chunk_sensitivity(layer, start, values, index, partials):
    inst, variables, radial, axial = values.shape
    surface = index.shape[1]
    place = index[...]
    lane = place % axial
    row = (place // axial) % radial
    select = lax.broadcasted_iota(jnp.int32, (axial, surface), 0) == jnp.broadcast_to(lane, (axial, surface))
    select = select.astype(jnp.float32).astype(jnp.bfloat16)
    here = (lax.broadcasted_iota(jnp.int32, (radial, surface), 0) == jnp.broadcast_to(row, (radial, surface))) & (
        jnp.broadcast_to(place // (axial * radial), (radial, surface)) == layer
    )
    flat = values[...].reshape(inst * variables * radial, axial)
    high = flat.astype(jnp.bfloat16)
    rest = flat - high.astype(jnp.float32)
    middle = rest.astype(jnp.bfloat16)
    low = (rest - middle.astype(jnp.float32)).astype(jnp.bfloat16)
    picked = jnp.dot(
        jnp.concatenate([high, middle, low], axis=1),
        jnp.concatenate([select, select, select], axis=0),
        preferred_element_type=jnp.float32,
    )
    sums = [jnp.zeros((radial, surface), jnp.float32) for _ in range(partials.shape[0])]
    for n in range(inst):
        for v in range(variables):
            at = (n * variables + v) * radial
            part = picked[at : at + radial]
            for k in range(len(sums)):
                sums[k] = sums[k] + part * jnp.broadcast_to(partials[k, v, start + n : start + n + 1, :], (radial, surface))
    return [jnp.sum(jnp.where(here, s, 0.0), axis=0, keepdims=True) for s in sums]


def own_layer(side):
    odd_block = lax.axis_index("blocks") % 2
    return odd_block if side else 1 - odd_block


def copy_all(pairs, sems):
    copies = [pltpu.make_async_copy(*pair, sems.at[j]) for j, pair in enumerate(pairs)]
    for copy in copies:
        copy.start()
    for copy in copies:
        copy.wait()


def layer_of(source, layer, out, start=0):
    return [(source.at[start + n, :, layer], out.at[n]) for n in range(out.shape[0])]


def first_split(source, out, sems):
    copy_all(layer_of(source, own_layer(0), out), sems)


def load_kernel(grad, diag, coupling, source, after, grad_out, diag_out, coupling_out, whole, *refs):
    *chunks, sems = refs
    layer = own_layer(1)
    pairs = layer_of(source, layer, whole)
    for j, chunk in enumerate(chunks):
        pairs += layer_of(source, layer, chunk, j * chunk.shape[0])
    copy_all(pairs + [(coupling, coupling_out), (grad, grad_out), (diag, diag_out)], sems)


def pack_kernel(even, odd, both):
    both[0] = even[...]
    both[1] = odd[...]


def join_kernel(*refs):
    *chunks, out, sems = refs
    pairs = []
    start = 0
    for chunk in chunks:
        layer = own_layer(0 if start < out.shape[0] else 1)
        first = start % out.shape[0]
        pairs.append((chunk, out.at[pl.ds(first, chunk.shape[0]), :, layer]))
        start += chunk.shape[0]
    copy_all(pairs, sems)


VMEM = pl.BlockSpec(memory_space=pltpu.VMEM)
HBM = pl.BlockSpec(memory_space=pltpu.HBM)
COST = pl.CostEstimate(flops=10**10, transcendentals=0, bytes_accessed=10**8)
PACK_COST = COST
PARAMS = pltpu.CompilerParams(vmem_limit_bytes=24 * 1024 * 1024)


def arrays(*shapes):
    return [jax.ShapeDtypeStruct(s, jnp.float32) for s in shapes]


def sweep_chunk(start, size, side, own, partner, inner, halo, fixed, after, earlier=()):
    def kernel(own, partner, inner, halo, grad, diag, coupling, *refs):
        *refs, masked, resid = refs[len(after) :]
        before, outs = refs[: len(earlier)], refs[len(earlier) :]
        new = outs[0]
        update_chunk(
            own_layer(side), start, own, partner.at[1 - lax.axis_index("inst"), side], inner, halo, grad, diag, coupling, new, masked, resid
        )
        if earlier:
            for j, chunk in enumerate([*before, new]):
                size = chunk.shape[0]
                outs[1][j * size : (j + 1) * size] = chunk[...]

    operands = (own, partner, inner, halo, *fixed, *after, *earlier)
    _, variables, radial, axial = own.shape
    shapes = [(size, variables, radial, axial)] + ([own.shape] if earlier else [])
    return pl.pallas_call(
        kernel,
        out_shape=arrays(*shapes),
        in_specs=[VMEM] * len(operands),
        out_specs=[VMEM] * len(shapes),
        scratch_shapes=[
            pltpu.VMEM((size, 4, radial, axial), jnp.float32),
            pltpu.VMEM((size, variables, radial, axial), jnp.float32),
        ],
        cost_estimate=COST,
        compiler_params=PARAMS,
    )(*operands)


def last_chunk(start, size, side, own, partner, inner, halo, fixed, index, partials, sens):
    def kernel(own, partner, inner, halo, grad, diag, coupling, index, partials, *refs):
        *before, new, out, masked, resid = refs
        layer = own_layer(side)
        update_chunk(layer, start, own, partner.at[1 - lax.axis_index("inst"), side], inner, halo, grad, diag, coupling, new, masked, resid)
        for k, row in enumerate(chunk_sensitivity(layer, start, new, index, partials)):
            out[k : k + 1, :] = before[0][k : k + 1, :] + row if before else row

    operands = (own, partner, inner, halo, *fixed, index, partials, *sens)
    _, variables, radial, axial = own.shape
    return pl.pallas_call(
        kernel,
        out_shape=arrays((size, variables, radial, axial), (partials.shape[0], index.shape[1])),
        in_specs=[VMEM] * len(operands),
        out_specs=[VMEM] * 2,
        scratch_shapes=[
            pltpu.VMEM((size, 4, radial, axial), jnp.float32),
            pltpu.VMEM((size, variables, radial, axial), jnp.float32),
        ],
        cost_estimate=COST,
        compiler_params=PARAMS,
    )(*operands)


def body(
    adjoint_start, objective_grad, diag_inverse, face_coupling, surface_index, wall_point_partials
):
    count = lax.axis_size("blocks")
    assert count % 2 == 0 and lax.axis_size("inst") == 2 and adjoint_start.shape[2] == 2
    inst, variables, _, radial, axial = adjoint_start.shape
    sizes = [inst // c for c in CHUNKS]
    even_pairs = [(i, i ^ 1) for i in range(count)]
    odd_pairs = [(i, (((i + 1) ^ 1) - 1) % count) for i in range(count)]
    index = surface_index.reshape(1, -1)
    partials = jnp.transpose(wall_point_partials, (1, 2, 0, 3))
    layer_shape = (inst, variables, radial, axial)

    def cores(values):
        return lax.ppermute(values, "inst", [(0, 1), (1, 0)])

    def exchange(whole):
        (both,) = pl.pallas_call(
            pack_kernel,
            out_shape=arrays((2,) + layer_shape),
            in_specs=[VMEM] * 2,
            out_specs=[VMEM],
            cost_estimate=PACK_COST,
            compiler_params=PARAMS,
        )(*whole)
        return lax.all_gather(both, "inst", axis=0)

    pairs = (even_pairs, odd_pairs)

    def swap(side, chunks):
        return [lax.ppermute(c, "blocks", pairs[side]) for c in chunks]

    (even,) = pl.pallas_call(
        first_split,
        out_shape=arrays(layer_shape),
        in_specs=[HBM],
        out_specs=[VMEM],
        scratch_shapes=[pltpu.SemaphoreType.DMA((inst,))],
        compiler_params=PARAMS,
    )(pltpu.with_memory_space_constraint(adjoint_start, pltpu.HBM))
    sources = (objective_grad, diag_inverse, face_coupling, adjoint_start)
    chunk_shapes = [(sizes[1],) + layer_shape[1:]] * (CHUNKS[1] if CHUNKS[1] > 1 else 0)
    *fixed, odd = pl.pallas_call(
        load_kernel,
        out_shape=arrays(*(s.shape for s in sources[:3]), layer_shape, *chunk_shapes),
        in_specs=[HBM] * len(sources) + [VMEM],
        out_specs=[VMEM] * (4 + len(chunk_shapes)),
        scratch_shapes=[pltpu.SemaphoreType.DMA((inst * (2 if chunk_shapes else 1) + 3,))],
        cost_estimate=COST,
        compiler_params=PARAMS,
    )(*(pltpu.with_memory_space_constraint(s, pltpu.HBM) for s in sources), even)
    fixed, odd, chunks = fixed[:3], (fixed + [odd])[3], (fixed + [odd])[4:]
    whole = [even, odd]
    halos = [swap(0, [even]) * CHUNKS[0], swap(1, chunks or [odd])]
    partner = exchange(whole)
    for sweep in range(SWEEPS - 1):
        next_halos, next_whole = [None, None], [None, None]
        for side, size in enumerate(sizes):
            done = []
            for j in range(CHUNKS[side]):
                args = (side, whole[side], partner, whole[1 - side], halos[side][j], fixed)
                after = next_whole[:side]
                new, *next_whole[side] = sweep_chunk(j * size, size, *args, after, done if (j + 1) * size == inst else ())
                done.append(new)
            next_halos[side] = swap(side, done)
            (next_whole[side],) = next_whole[side] or done
        halos, whole = next_halos, next_whole
        partner = exchange(whole)
    sens = ()
    done = []
    for side, size in enumerate(sizes):
        for j in range(CHUNKS[side]):
            args = (side, whole[side], partner, whole[1 - side], halos[side][j], fixed)
            new, *sens = last_chunk(j * size, size, *args, index, partials, sens)
            done.append(new)
    (total,) = sens
    (adjoint,) = pl.pallas_call(
        join_kernel,
        out_shape=arrays(adjoint_start.shape),
        in_specs=[VMEM] * len(done),
        out_specs=[HBM],
        scratch_shapes=[pltpu.SemaphoreType.DMA((len(done),))],
        compiler_params=PARAMS,
    )(*done)
    return adjoint, total + cores(total)


def solution(mesh):
    return jax.shard_map(
        body,
        mesh=mesh,
        in_specs=(
            P(("groups", "inst"), None, "blocks", None, None),
            P(("groups", "inst"), None, "blocks", None, None),
            P(("groups", "inst"), None, None, "blocks", None, None),
            P(("groups", "inst"), None, "blocks", None, None),
            P(("groups", "blocks")),
            P(("groups", "inst"), None, None, "blocks"),
        ),
        out_specs=(
            P(("groups", "inst"), None, "blocks", None, None),
            P(None, ("groups", "blocks")),
        ),
        check_vma=False,
    )
```

time: 58.1 us -> 47.2 us (0.81)
  waiting for transfers between devices: 21 us -> 4.23 us
  blocking collectives: 0 us -> 9.44 us
  local copies, waits for them, and re-layouts: 4.79 us -> 0.01 us
  Pallas kernels: 4 us -> 7.35 us
  starting transfers between devices: 26.7 us -> 24.6 us
    ppermute x17 -> x9, waiting for transfers between devices: 21 us -> 4.23 us  [the longest x8 3.86 us: swap(): return [lax.ppermute(c, 'blocks', pairs[side]) for c in chunks]]
    all_gather x0 -> x4, blocking collectives: none -> 9.44 us  [exchange(): return lax.all_gather(both, 'inst', axis=0)]
    unnamed x16 -> x4, local copies, waits for them, and re-layouts: 3.68 us -> 0.01 us
    pallas_call x8 -> x15, Pallas kernels: 4 us -> 7.35 us  [the longest x6 2.22 us: sweep_chunk(): pl.pallas_call(kernel, out_shape=arrays(*shapes), in_specs=[VMEM] * len(o...]
    ppermute x17 -> x9, starting transfers between devices: 26.7 us -> 24.6 us  [the longest x8 24.5 us: swap(): return [lax.ppermute(c, 'blocks', pairs[side]) for c in chunks]]
    squeeze x1 -> x0, local copies, waits for them, and re-layouts: 1.1 us -> none  [body(): lax.dynamic_index_in_dim(adjoint_start, even_layer, 2, keepdims=False)]
  transfers between devices with their start and end apart: 17 -> 9, of which waited for: 6 -> 5; matrix products, arithmetic and copies ran while one was open for 0% -> 0% of each run, Pallas kernels for 5% -> 12%
where the time goes in v2:
time: 47.2 us; the launch traced here: 46.9 us
  starting transfers between devices  24.6 us (52%)
  blocking collectives  9.44 us (20%)
  Pallas kernels  7.35 us (16%)
  waiting for transfers between devices  4.23 us (9%)
  between operations  0.76 us (2%)
  other arithmetic  0.6 us (1%)
    ppermute x8, starting transfers between devices, swap(): return [lax.ppermute(c, 'blocks', pairs[side]) for c in chunks]  24.5 us
    all_gather x4, blocking collectives, exchange(): return lax.all_gather(both, 'inst', axis=0)  9.44 us
    ppermute x8, waiting for transfers between devices, swap(): return [lax.ppermute(c, 'blocks', pairs[side]) for c in chunks]  3.86 us
    pallas_call x6, Pallas kernels, sweep_chunk(): pl.pallas_call(kernel, out_shape=arrays(*shapes), in_specs=[VMEM] * len(o...  2.22 us
    pallas_call x1, Pallas kernels, body(): pl.pallas_call(load_kernel, out_shape=arrays(*(s.shape for s in sources[:...  2.14 us
    pallas_call x2, Pallas kernels, last_chunk(): pl.pallas_call(kernel, out_shape=arrays((size, variables, radial, axial),...  1.17 us
    pallas_call x1, Pallas kernels, body(): pl.pallas_call(first_split, out_shape=arrays(layer_shape), in_specs=[HBM]...  0.95 us
  transfers between devices with their start and end apart: 9, of which 5 were waited for; matrix products, arithmetic and copies ran while one was open for 0% of the time, Pallas kernels for 12%

profile of v2, /device:TPU:0, one launch (start us, length us, event | category | flops | bytes accessed | tf_op | source)
XLA Modules:
  0.0 46.9 jit_solution(12950824164309889637)
XLA Ops:
  0.6 0.9 %shard_map.77.after.even.own.inner = f32[8,6,8,128]{3,2,1,0:T(8,128)S(1)} custom-call(f32[8,6,2,8,128]{4,3,2,1,0:T(8,128)} %source.3), custom_call_target="tpu_custom_call" | custom-call | tf_op jit(solution)/shard_map/pallas_call | solution.py:234
  1.6 3.0 %collective-permute-start = (f32[8,6,8,128]{3,2,1,0:T(8,128)S(1)}, f32[8,6,8,128]{3,2,1,0:T(8,128)S(1)}, u32[]{:S(2)}, u32[]{:S(2)}) collective-permute-start(f32[8,6,8,128]{3,2,1,0:T(8,128)S(1)} %shard_map.77.after.even.own.inner), channel_id=1, source_target_pairs={{0,2},{2,0},{4,6},{6,4},{8,10},{10,8},{12,14},{14,12},{1,3},{3,1},... | collective-permute-start | bytes 589832 | tf_op jit(solution)/shard_map/ppermute | solution.py:232
  4.6 2.1 %shard_map.78 = (f32[8,6,2,8,128]{4,3,2,1,0:T(8,128)S(1)}, f32[8,6,6,2,8,128]{5,4,3,2,1,0:T(8,128)S(1)}, f32[8,6,2,8,128]{4,3,2,1,0:T(8,128)S(1)}, f32[8,6,8,128]{3,2,1,0:T(8,128)S(1)}) custom-call(f32[8,6,2,8,128]{4,3,2,1,0:T(8,128)} %grad.1, f32[8,6,6,2,8,128]{5,4,3,2,1,0:T(8,128)} %diag.1, f32[8,6,2,8,128]{4,3,2,1,0:T(8,128)} %coupling.1, ...), custom_call_target="tpu_custom_call" | custom-call | flops 10000000000 | bytes 100000000 | tf_op jit(solution)/shard_map/pallas_call | solution.py:244
  6.7 3.6 %collective-permute-start.1 = (f32[8,6,8,128]{3,2,1,0:T(8,128)S(1)}, f32[8,6,8,128]{3,2,1,0:T(8,128)S(1)}, u32[]{:S(2)}, u32[]{:S(2)}) collective-permute-start(f32[8,6,8,128]{3,2,1,0:T(8,128)S(1)} %get-tuple-element.10.odd.inner.own), channel_id=1, source_target_pairs={{0,14},{2,4},{4,2},{6,8},{8,6},{10,12},{12,10},{14,0},{1,15},{3,5}... | collective-permute-start | bytes 589832 | tf_op jit(solution)/shard_map/ppermute | solution.py:232
  10.4 2.4 %all-gather = f32[4,8,6,8,128]{4,3,2,1,0:T(8,128)S(1)} all-gather(f32[2,8,6,8,128]{4,3,2,1,0:T(8,128)S(1)} %shard_map.79), channel_id=2, replica_groups=mesh['groups'=2,'blocks'=8,'inst'=2] {'inst'}, dimensions={0}, use_global_device_ids=true | all-gather | bytes 1179648 | tf_op jit(solution)/shard_map/all_gather | solution.py:227
  12.8 0.2 collective-permute-done.halo
  13.0 0.4 shard_map.80.refs_0_.even.own.inner
  13.4 2.5 %collective-permute-start.2 = (f32[8,6,8,128]{3,2,1,0:T(8,128)S(1)}, f32[8,6,8,128]{3,2,1,0:T(8,128)S(1)}, u32[]{:S(2)}, u32[]{:S(2)}) collective-permute-start(f32[8,6,8,128]{3,2,1,0:T(8,128)S(1)} %shard_map.80.refs_0_.even.own.inner), channel_id=1, source_target_pairs={{0,2},{2,0},{4,6},{6,4},{8,10},{10,8},{12,14},{14,12},{1,3},{3,1},... | collective-permute-start | bytes 589832 | tf_op jit(solution)/shard_map/ppermute | solution.py:232
  15.9 0.0 collective-permute-done.1.halo
  15.9 0.3 shard_map.81.odd.inner.own
  16.2 3.8 %collective-permute-start.3 = (f32[8,6,8,128]{3,2,1,0:T(8,128)S(1)}, f32[8,6,8,128]{3,2,1,0:T(8,128)S(1)}, u32[]{:S(2)}, u32[]{:S(2)}) collective-permute-start(f32[8,6,8,128]{3,2,1,0:T(8,128)S(1)} %shard_map.81.odd.inner.own), channel_id=1, source_target_pairs={{0,14},{2,4},{4,2},{6,8},{8,6},{10,12},{12,10},{14,0},{1,15},{3,5}... | collective-permute-start | bytes 589832 | tf_op jit(solution)/shard_map/ppermute | solution.py:232
  20.0 2.4 %all-gather.1 = f32[4,8,6,8,128]{4,3,2,1,0:T(8,128)S(1)} all-gather(f32[2,8,6,8,128]{4,3,2,1,0:T(8,128)S(1)} %shard_map.82), channel_id=3, replica_groups=mesh['groups'=2,'blocks'=8,'inst'=2] {'inst'}, dimensions={0}, use_global_device_ids=true | all-gather | bytes 1179648 | tf_op jit(solution)/shard_map/all_gather | solution.py:227
  22.4 0.6 %collective-permute-done.2.halo = f32[8,6,8,128]{3,2,1,0:T(8,128)S(1)} collective-permute-done((f32[8,6,8,128]{3,2,1,0:T(8,128)S(1)}, f32[8,6,8,128]{3,2,1,0:T(8,128)S(1)}, u32[]{:S(2)}, u32[]{:S(2)}) %collective-permute-start.2) | collective-permute-done | bytes 196640 | tf_op jit(solution)/shard_map/ppermute | solution.py:232
  22.9 0.4 shard_map.83.refs_0_.even.own.inner
  23.3 2.5 %collective-permute-start.4 = (f32[8,6,8,128]{3,2,1,0:T(8,128)S(1)}, f32[8,6,8,128]{3,2,1,0:T(8,128)S(1)}, u32[]{:S(2)}, u32[]{:S(2)}) collective-permute-start(f32[8,6,8,128]{3,2,1,0:T(8,128)S(1)} %shard_map.83.refs_0_.even.own.inner), channel_id=1, source_target_pairs={{0,2},{2,0},{4,6},{6,4},{8,10},{10,8},{12,14},{14,12},{1,3},{3,1},... | collective-permute-start | bytes 589832 | tf_op jit(solution)/shard_map/ppermute | solution.py:232
  25.8 0.0 collective-permute-done.3.halo
  25.8 0.3 shard_map.84.odd.inner.own
  26.2 2.7 %collective-permute-start.5 = (f32[8,6,8,128]{3,2,1,0:T(8,128)S(1)}, f32[8,6,8,128]{3,2,1,0:T(8,128)S(1)}, u32[]{:S(2)}, u32[]{:S(2)}) collective-permute-start(f32[8,6,8,128]{3,2,1,0:T(8,128)S(1)} %shard_map.84.odd.inner.own), channel_id=1, source_target_pairs={{0,14},{2,4},{4,2},{6,8},{8,6},{10,12},{12,10},{14,0},{1,15},{3,5}... | collective-permute-start | bytes 589832 | tf_op jit(solution)/shard_map/ppermute | solution.py:232
  28.9 2.4 %all-gather.2 = f32[4,8,6,8,128]{4,3,2,1,0:T(8,128)S(1)} all-gather(f32[2,8,6,8,128]{4,3,2,1,0:T(8,128)S(1)} %shard_map.85), channel_id=4, replica_groups=mesh['groups'=2,'blocks'=8,'inst'=2] {'inst'}, dimensions={0}, use_global_device_ids=true | all-gather | bytes 1179648 | tf_op jit(solution)/shard_map/all_gather | solution.py:227
  31.2 1.6 %collective-permute-done.4.halo = f32[8,6,8,128]{3,2,1,0:T(8,128)S(1)} collective-permute-done((f32[8,6,8,128]{3,2,1,0:T(8,128)S(1)}, f32[8,6,8,128]{3,2,1,0:T(8,128)S(1)}, u32[]{:S(2)}, u32[]{:S(2)}) %collective-permute-start.4) | collective-permute-done | bytes 196640 | tf_op jit(solution)/shard_map/ppermute | solution.py:232
  32.8 0.4 shard_map.86.refs_0_.even.own.inner
  33.2 2.5 %collective-permute-start.6 = (f32[8,6,8,128]{3,2,1,0:T(8,128)S(1)}, f32[8,6,8,128]{3,2,1,0:T(8,128)S(1)}, u32[]{:S(2)}, u32[]{:S(2)}) collective-permute-start(f32[8,6,8,128]{3,2,1,0:T(8,128)S(1)} %shard_map.86.refs_0_.even.own.inner), channel_id=1, source_target_pairs={{0,2},{2,0},{4,6},{6,4},{8,10},{10,8},{12,14},{14,12},{1,3},{3,1},... | collective-permute-start | bytes 589832 | tf_op jit(solution)/shard_map/ppermute | solution.py:232
  35.7 0.0 collective-permute-done.5.halo
  35.7 0.3 shard_map.87.odd.inner.own
  36.1 0.0 copy-start
  36.1 0.0 copy-start.1
  36.1 3.9 %collective-permute-start.7 = (f32[8,6,8,128]{3,2,1,0:T(8,128)S(1)}, f32[8,6,8,128]{3,2,1,0:T(8,128)S(1)}, u32[]{:S(2)}, u32[]{:S(2)}) collective-permute-start(f32[8,6,8,128]{3,2,1,0:T(8,128)S(1)} %shard_map.87.odd.inner.own), channel_id=1, source_target_pairs={{0,14},{2,4},{4,2},{6,8},{8,6},{10,12},{12,10},{14,0},{1,15},{3,5}... | collective-permute-start | bytes 589832 | tf_op jit(solution)/shard_map/ppermute | solution.py:232
  40.0 2.4 %all-gather.3 = f32[4,8,6,8,128]{4,3,2,1,0:T(8,128)S(1)} all-gather(f32[2,8,6,8,128]{4,3,2,1,0:T(8,128)S(1)} %shard_map.88), channel_id=5, replica_groups=mesh['groups'=2,'blocks'=8,'inst'=2] {'inst'}, dimensions={0}, use_global_device_ids=true | all-gather | bytes 1179648 | tf_op jit(solution)/shard_map/all_gather | solution.py:227
  42.4 0.0 collective-permute-done.6.halo
  42.4 0.0 copy-done
  42.4 0.0 copy-done.1
  42.4 0.6 %shard_map.89 = (f32[8,6,8,128]{3,2,1,0:T(8,128)S(1)}, f32[3,256]{1,0:T(4,128)S(1)}) custom-call(f32[8,6,8,128]{3,2,1,0:T(8,128)S(1)} %shard_map.86.refs_0_.even.own.inner, f32[2,2,8,6,8,128]{5,4,3,2,1,0:T(8,128)S(1)} %bitcast.6, f32[8,6,8,128]{3,2,1,0:T(8,128)S(1)} %shard_map.87.odd.inner.own, f32[8,6,8,128]{3,2,1,0:T(8,128)S(1)} %collective-permute-done.6.halo, ...), custom_call_target="tpu_custom_call" | custom-call | flops 10000000000 | bytes 100000000 | tf_op jit(solution)/shard_map/pallas_call | solution.py:188
  43.0 1.5 %collective-permute-done.7.halo = f32[8,6,8,128]{3,2,1,0:T(8,128)S(1)} collective-permute-done((f32[8,6,8,128]{3,2,1,0:T(8,128)S(1)}, f32[8,6,8,128]{3,2,1,0:T(8,128)S(1)}, u32[]{:S(2)}, u32[]{:S(2)}) %collective-permute-start.7) | collective-permute-done | bytes 196640 | tf_op jit(solution)/shard_map/ppermute | solution.py:232
  44.5 0.6 %shard_map.90 = (f32[8,6,8,128]{3,2,1,0:T(8,128)S(1)}, f32[3,256]{1,0:T(4,128)S(1)}) custom-call(f32[8,6,8,128]{3,2,1,0:T(8,128)S(1)} %shard_map.87.odd.inner.own, f32[2,2,8,6,8,128]{5,4,3,2,1,0:T(8,128)S(1)} %bitcast.7, f32[8,6,8,128]{3,2,1,0:T(8,128)S(1)} %shard_map.86.refs_0_.even.own.inner, f32[8,6,8,128]{3,2,1,0:T(8,128)S(1)} %collective-permute-done.7.halo, ...), custom_call_target="tpu_custom_call" | custom-call | flops 10000000000 | bytes 100000000 | tf_op jit(solution)/shard_map/pallas_call | solution.py:188
  45.1 0.1 collective-permute-start.8
  45.2 0.8 %shard_map.91 = f32[8,6,2,8,128]{4,3,2,1,0:T(8,128)} custom-call(f32[8,6,8,128]{3,2,1,0:T(8,128)S(1)} %get-tuple-element.14.refs_0_, f32[8,6,8,128]{3,2,1,0:T(8,128)S(1)} %get-tuple-element.16.refs_1_), custom_call_target="tpu_custom_call" | custom-call | tf_op jit(solution)/shard_map/pallas_call | solution.py:278
  46.0 0.4 collective-permute-done.8
  46.4 0.6 %add.3 = f32[3,256]{1,0:T(4,128)} add(f32[3,256]{1,0:T(4,128)S(1)} %get-tuple-element.17, f32[3,256]{1,0:T(4,128)S(1)} %collective-permute-done.8) | non-fusion elementwise | flops 768 | bytes 9216 | tf_op jit(solution)/shard_map/add | solution.py:286
  (4 shorter events, 0.1 us)
Async XLA Ops:
  1.6 11.4 %collective-permute-start = (f32[8,6,8,128]{3,2,1,0:T(8,128)S(1)}, f32[8,6,8,128]{3,2,1,0:T(8,128)S(1)}, u32[]{:S(2)}, u32[]{:S(2)}) collective-permute-start(f32[8,6,8,128]{3,2,1,0:T(8,128)S(1)} %shard_map.77.after.even.own.inner), channel_id=1, source_target_pairs={{0,2},{2,0},{4,6},{6,4},{8,10},{10,8},{12,14},{14,12},{1,3},{3,1},... | collective-permute-start | bytes 589832 | tf_op jit(solution)/shard_map/ppermute | solution.py:232
  6.7 9.1 %collective-permute-start.1 = (f32[8,6,8,128]{3,2,1,0:T(8,128)S(1)}, f32[8,6,8,128]{3,2,1,0:T(8,128)S(1)}, u32[]{:S(2)}, u32[]{:S(2)}) collective-permute-start(f32[8,6,8,128]{3,2,1,0:T(8,128)S(1)} %get-tuple-element.10.odd.inner.own), channel_id=1, source_target_pairs={{0,14},{2,4},{4,2},{6,8},{8,6},{10,12},{12,10},{14,0},{1,15},{3,5}... | collective-permute-start | bytes 589832 | tf_op jit(solution)/shard_map/ppermute | solution.py:232
  13.4 9.6 %collective-permute-start.2 = (f32[8,6,8,128]{3,2,1,0:T(8,128)S(1)}, f32[8,6,8,128]{3,2,1,0:T(8,128)S(1)}, u32[]{:S(2)}, u32[]{:S(2)}) collective-permute-start(f32[8,6,8,128]{3,2,1,0:T(8,128)S(1)} %shard_map.80.refs_0_.even.own.inner), channel_id=1, source_target_pairs={{0,2},{2,0},{4,6},{6,4},{8,10},{10,8},{12,14},{14,12},{1,3},{3,1},... | collective-permute-start | bytes 589832 | tf_op jit(solution)/shard_map/ppermute | solution.py:232
  16.2 9.6 %collective-permute-start.3 = (f32[8,6,8,128]{3,2,1,0:T(8,128)S(1)}, f32[8,6,8,128]{3,2,1,0:T(8,128)S(1)}, u32[]{:S(2)}, u32[]{:S(2)}) collective-permute-start(f32[8,6,8,128]{3,2,1,0:T(8,128)S(1)} %shard_map.81.odd.inner.own), channel_id=1, source_target_pairs={{0,14},{2,4},{4,2},{6,8},{8,6},{10,12},{12,10},{14,0},{1,15},{3,5}... | collective-permute-start | bytes 589832 | tf_op jit(solution)/shard_map/ppermute | solution.py:232
  23.3 9.5 %collective-permute-start.4 = (f32[8,6,8,128]{3,2,1,0:T(8,128)S(1)}, f32[8,6,8,128]{3,2,1,0:T(8,128)S(1)}, u32[]{:S(2)}, u32[]{:S(2)}) collective-permute-start(f32[8,6,8,128]{3,2,1,0:T(8,128)S(1)} %shard_map.83.refs_0_.even.own.inner), channel_id=1, source_target_pairs={{0,2},{2,0},{4,6},{6,4},{8,10},{10,8},{12,14},{14,12},{1,3},{3,1},... | collective-permute-start | bytes 589832 | tf_op jit(solution)/shard_map/ppermute | solution.py:232
  26.2 9.5 %collective-permute-start.5 = (f32[8,6,8,128]{3,2,1,0:T(8,128)S(1)}, f32[8,6,8,128]{3,2,1,0:T(8,128)S(1)}, u32[]{:S(2)}, u32[]{:S(2)}) collective-permute-start(f32[8,6,8,128]{3,2,1,0:T(8,128)S(1)} %shard_map.84.odd.inner.own), channel_id=1, source_target_pairs={{0,14},{2,4},{4,2},{6,8},{8,6},{10,12},{12,10},{14,0},{1,15},{3,5}... | collective-permute-start | bytes 589832 | tf_op jit(solution)/shard_map/ppermute | solution.py:232
  33.2 9.2 %collective-permute-start.6 = (f32[8,6,8,128]{3,2,1,0:T(8,128)S(1)}, f32[8,6,8,128]{3,2,1,0:T(8,128)S(1)}, u32[]{:S(2)}, u32[]{:S(2)}) collective-permute-start(f32[8,6,8,128]{3,2,1,0:T(8,128)S(1)} %shard_map.86.refs_0_.even.own.inner), channel_id=1, source_target_pairs={{0,2},{2,0},{4,6},{6,4},{8,10},{10,8},{12,14},{14,12},{1,3},{3,1},... | collective-permute-start | bytes 589832 | tf_op jit(solution)/shard_map/ppermute | solution.py:232
  36.1 6.3 %copy-start = (f32[8,3,6,256]{3,0,2,1:T(8,128)S(1)}, f32[8,3,6,256]{3,0,2,1:T(8,128)}, u32[]{:S(2)}) copy-start(f32[8,3,6,256]{3,0,2,1:T(8,128)} %param.11) | copy-start | bytes 442372
  36.1 6.3 %copy-start.1 = (s32[256]{0:T(256)S(1)}, s32[256]{0:T(256)}, u32[]{:S(2)}) copy-start(s32[256]{0:T(256)} %param.10) | copy-start | bytes 3076
  36.1 8.4 %collective-permute-start.7 = (f32[8,6,8,128]{3,2,1,0:T(8,128)S(1)}, f32[8,6,8,128]{3,2,1,0:T(8,128)S(1)}, u32[]{:S(2)}, u32[]{:S(2)}) collective-permute-start(f32[8,6,8,128]{3,2,1,0:T(8,128)S(1)} %shard_map.87.odd.inner.own), channel_id=1, source_target_pairs={{0,14},{2,4},{4,2},{6,8},{8,6},{10,12},{12,10},{14,0},{1,15},{3,5}... | collective-permute-start | bytes 589832 | tf_op jit(solution)/shard_map/ppermute | solution.py:232
  45.1 1.2 %collective-permute-start.8 = (f32[3,256]{1,0:T(4,128)S(1)}, f32[3,256]{1,0:T(4,128)S(1)}, u32[]{:S(2)}, u32[]{:S(2)}) collective-permute-start(f32[3,256]{1,0:T(4,128)S(1)} %get-tuple-element.17), channel_id=1, source_target_pairs={{0,1},{1,0},{2,3},{3,2},{4,5},{5,4},{6,7},{7,6},{8,9},{9,8},{10,11... | collective-permute-start | bytes 9224 | tf_op jit(solution)/shard_map/ppermute | solution.py:216

commit v3 on v1

v3 whole, which is shorter than its diff:
```python
import math

import jax
import jax.numpy as jnp
from jax import lax
from jax.experimental import pallas as pl
from jax.experimental.pallas import tpu as pltpu
from jax.sharding import PartitionSpec as P

SWEEPS = 4
SPECTRAL_WEIGHT = 0.25


def spectral_values(number):
    values = [0.0]
    for k in range(1, number):
        angle = math.pi * k / number
        values.append(SPECTRAL_WEIGHT * 0.5 * (-1) ** k * math.cos(angle) / math.sin(angle))
    return values


def local_terms(layer, own, partner, inner, grad, coupling, base, masked):
    inst, variables, radial, axial = own.shape
    values = spectral_values(2 * inst)
    rows = lax.broadcasted_iota(jnp.int32, (radial, axial), 0)
    lanes = lax.broadcasted_iota(jnp.int32, (radial, axial), 1)
    edges = (rows > 0, rows < radial - 1, lanes > 0, lanes < axial - 1)
    for n in range(inst):
        for d, inside in enumerate(edges):
            masked[n, d] = jnp.where(inside, coupling[n, 2 + d, layer], 0.0)
    for u in range(variables):
        cycle = [own[m, u] for m in range(inst)] + [partner[m, u] for m in range(inst)]
        for n in range(inst):
            center = cycle[n]
            total = grad[n, u, layer]
            total = total + coupling[n, 1 - layer, layer] * inner[n, u]
            total = total + masked[n, 0] * pltpu.roll(center, 1, 0)
            total = total + masked[n, 1] * pltpu.roll(center, radial - 1, 0)
            total = total + masked[n, 2] * pltpu.roll(center, 1, 1)
            total = total + masked[n, 3] * pltpu.roll(center, axial - 1, 1)
            term = values[inst] * cycle[n + inst]
            for k in range(1, inst):
                term = term + values[k] * (cycle[(n + k) % (2 * inst)] - cycle[(n - k) % (2 * inst)])
            base[n, u] = total - term


def update_layer(layer, base, halo, diag, coupling, new):
    inst, variables = base.shape[:2]
    for n in range(inst):
        weight = coupling[n, layer, layer]
        terms = [base[n, u] + weight * halo[n, u] for u in range(variables)]
        for v in range(variables):
            total = diag[n, 0, v, layer] * terms[0]
            for u in range(1, variables):
                total = total + diag[n, u, v, layer] * terms[u]
            new[n, v] = total


def layer_sensitivity(layer, values, index, partials):
    inst, variables, radial, axial = values.shape
    surface = index.shape[1]
    place = index[...]
    lane = place % axial
    row = (place // axial) % radial
    select = lax.broadcasted_iota(jnp.int32, (axial, surface), 0) == jnp.broadcast_to(lane, (axial, surface))
    select = select.astype(jnp.float32).astype(jnp.bfloat16)
    here = (lax.broadcasted_iota(jnp.int32, (radial, surface), 0) == jnp.broadcast_to(row, (radial, surface))) & (
        jnp.broadcast_to(place // (axial * radial), (radial, surface)) == layer
    )
    flat = values[...].reshape(inst * variables * radial, axial)
    high = flat.astype(jnp.bfloat16)
    rest = flat - high.astype(jnp.float32)
    middle = rest.astype(jnp.bfloat16)
    low = (rest - middle.astype(jnp.float32)).astype(jnp.bfloat16)
    picked = jnp.dot(
        jnp.concatenate([high, middle, low], axis=1),
        jnp.concatenate([select, select, select], axis=0),
        preferred_element_type=jnp.float32,
    )
    sums = [jnp.zeros((radial, surface), jnp.float32) for _ in range(partials.shape[0])]
    for n in range(inst):
        for v in range(variables):
            at = (n * variables + v) * radial
            part = picked[at : at + radial]
            for k in range(len(sums)):
                sums[k] = sums[k] + part * jnp.broadcast_to(partials[k, v, n : n + 1, :], (radial, surface))
    return [jnp.sum(jnp.where(here, s, 0.0), axis=0, keepdims=True) for s in sums]


def own_layer(side):
    odd_block = lax.axis_index("blocks") % 2
    return odd_block if side else 1 - odd_block


def copy_all(pairs, sems):
    copies = [pltpu.make_async_copy(*pair, sems.at[j]) for j, pair in enumerate(pairs)]
    for copy in copies:
        copy.start()
    for copy in copies:
        copy.wait()


def layer_of(source, side, out):
    return [(source.at[n, :, own_layer(side)], out.at[n]) for n in range(out.shape[0])]


def first_kernel(source, even, sems):
    copy_all(layer_of(source, 0, even), sems)


def load_kernel(grad, diag, coupling, source, after, grad_out, diag_out, coupling_out, odd, sems):
    pairs = [(coupling, coupling_out), (grad, grad_out), (diag, diag_out)]
    copy_all(layer_of(source, 1, odd) + pairs, sems)


def pack_kernel(even, odd, both):
    both[0] = even[...]
    both[1] = odd[...]


def join_kernel(even, odd, out, sems):
    copy_all([(layer, out.at[:, :, own_layer(side)]) for side, layer in enumerate((even, odd))], sems)


VMEM = pl.BlockSpec(memory_space=pltpu.VMEM)
HBM = pl.BlockSpec(memory_space=pltpu.HBM)
COST = pl.CostEstimate(flops=10**10, transcendentals=0, bytes_accessed=10**8)
PARAMS = pltpu.CompilerParams(vmem_limit_bytes=24 * 1024 * 1024)


def call(kernel, shapes, in_specs, operands, scratch=(), out_spec=VMEM):
    return pl.pallas_call(
        kernel,
        out_shape=[jax.ShapeDtypeStruct(s, jnp.float32) for s in shapes],
        in_specs=in_specs,
        out_specs=[out_spec] * len(shapes),
        scratch_shapes=list(scratch),
        cost_estimate=COST,
        compiler_params=PARAMS,
    )(*operands)


def local_kernel(even, odd, both, grad, coupling, base, masked):
    partner = both.at[1 - lax.axis_index("inst"), 0]
    local_terms(own_layer(0), even, partner, odd, grad, coupling, base, masked)


def even_layer(base, halo, fixed, last=None):
    _, diag, coupling = fixed

    def kernel(base, halo, diag, coupling, *refs):
        layer = own_layer(0)
        if last is None:
            (new,) = refs
        else:
            index, partials, new, sens = refs
        update_layer(layer, base, halo, diag, coupling, new)
        if last is not None:
            for k, row in enumerate(layer_sensitivity(layer, new, index, partials)):
                sens[k : k + 1, :] = row

    operands = (base, halo, diag, coupling, *(last or ()))
    shapes = [base.shape] + ([] if last is None else [(last[1].shape[0], last[0].shape[1])])
    return call(kernel, shapes, [VMEM] * len(operands), operands)


def odd_layer(odd, both, even, halo, fixed, after=(), last=None):
    def kernel(odd, both, even, halo, grad, diag, coupling, *refs):
        *refs, masked, base = refs[len(after) :]
        layer = own_layer(1)
        partner = both.at[1 - lax.axis_index("inst"), 1]
        if last is None:
            (new,) = refs
        else:
            index, partials, before, new, sens = refs
        local_terms(layer, odd, partner, even, grad, coupling, base, masked)
        update_layer(layer, base, halo, diag, coupling, new)
        if last is not None:
            for k, row in enumerate(layer_sensitivity(layer, new, index, partials)):
                sens[k : k + 1, :] = before[k : k + 1, :] + row

    operands = (odd, both, even, halo, *fixed, *after, *(last or ()))
    inst, _, radial, axial = odd.shape
    shapes = [odd.shape] + ([] if last is None else [last[2].shape])
    scratch = [pltpu.VMEM((inst, 4, radial, axial), jnp.float32), pltpu.VMEM(odd.shape, jnp.float32)]
    return call(kernel, shapes, [VMEM] * len(operands), operands, scratch)


def body(
    adjoint_start, objective_grad, diag_inverse, face_coupling, surface_index, wall_point_partials
):
    count = lax.axis_size("blocks")
    assert count % 2 == 0 and lax.axis_size("inst") == 2 and adjoint_start.shape[2] == 2
    inst, variables, _, radial, axial = adjoint_start.shape
    shape = (inst, variables, radial, axial)
    even_pairs = [(i, i ^ 1) for i in range(count)]
    odd_pairs = [(i, (((i + 1) ^ 1) - 1) % count) for i in range(count)]
    index = surface_index.reshape(1, -1)
    partials = jnp.transpose(wall_point_partials, (1, 2, 0, 3))

    def even_swap(layer):
        return lax.ppermute(layer, "blocks", even_pairs)

    def odd_swap(layer):
        return lax.ppermute(layer, "blocks", odd_pairs)

    def cores(values):
        return lax.all_gather(values, "inst", axis=0)

    def in_hbm(values):
        return pltpu.with_memory_space_constraint(values, pltpu.HBM)

    def exchange(even, odd):
        return cores(*call(pack_kernel, [(2,) + shape], [VMEM] * 2, [even, odd]))

    def local(even, odd, both):
        operands = (even, odd, both, fixed[0], fixed[2])
        masked = pltpu.VMEM((inst, 4, radial, axial), jnp.float32)
        return call(local_kernel, [shape], [VMEM] * 5, operands, [masked])[0]

    copies = [pltpu.SemaphoreType.DMA((inst + 3,))]
    start = in_hbm(adjoint_start)
    (even,) = call(first_kernel, [shape], [HBM], [start], copies)
    even_halo = even_swap(even)
    sources = (objective_grad, diag_inverse, face_coupling)
    *fixed, odd = call(
        load_kernel,
        [s.shape for s in sources] + [shape],
        [HBM] * 4 + [VMEM],
        [*map(in_hbm, sources), start, even],
        copies,
    )
    odd_halo = odd_swap(odd)
    both = exchange(even, odd)
    for sweep in range(SWEEPS - 1):
        base = local(even, odd, both)
        (new_even,) = even_layer(base, even_halo, fixed)
        even_halo = even_swap(new_even)
        (odd,) = odd_layer(odd, both, even, odd_halo, fixed, [new_even])
        odd_halo = odd_swap(odd)
        even = new_even
        both = exchange(even, odd)
    last = index, partials
    new_even, sens = even_layer(local(even, odd, both), even_halo, fixed, last)
    odd, sens = odd_layer(odd, both, even, odd_halo, fixed, (), last + (sens,))
    even = new_even
    (adjoint,) = call(join_kernel, [adjoint_start.shape], [VMEM] * 2, [even, odd], copies, HBM)
    return adjoint, sens + lax.ppermute(sens, "inst", [(0, 1), (1, 0)])


def solution(mesh):
    return jax.shard_map(
        body,
        mesh=mesh,
        in_specs=(
            P(("groups", "inst"), None, "blocks", None, None),
            P(("groups", "inst"), None, "blocks", None, None),
            P(("groups", "inst"), None, None, "blocks", None, None),
            P(("groups", "inst"), None, "blocks", None, None),
            P(("groups", "blocks")),
            P(("groups", "inst"), None, None, "blocks"),
        ),
        out_specs=(
            P(("groups", "inst"), None, "blocks", None, None),
            P(None, ("groups", "blocks")),
        ),
        check_vma=False,
    )
```

time: 58.1 us -> 47 us (0.81)
  waiting for transfers between devices: 21 us -> 3.4 us
  blocking collectives: 0 us -> 9.44 us
  local copies, waits for them, and re-layouts: 4.79 us -> 0.65 us
  Pallas kernels: 4 us -> 7.33 us
  starting transfers between devices: 26.7 us -> 24.5 us
    ppermute x17 -> x9, waiting for transfers between devices: 21 us -> 3.4 us  [the longest x4 1.62 us: even_swap(): return lax.ppermute(layer, 'blocks', even_pairs)]
    all_gather x0 -> x4, blocking collectives: none -> 9.44 us  [cores(): return lax.all_gather(values, 'inst', axis=0)]
    pallas_call x8 -> x19, Pallas kernels: 4 us -> 7.33 us  [call(): pl.pallas_call(kernel, out_shape=[jax.ShapeDtypeStruct(s, jnp.float32) fo...]
    unnamed x16 -> x4, local copies, waits for them, and re-layouts: 3.68 us -> 0.65 us
    ppermute x17 -> x9, starting transfers between devices: 26.7 us -> 24.5 us  [the longest x4 14 us: odd_swap(): return lax.ppermute(layer, 'blocks', odd_pairs)]
    squeeze x1 -> x0, local copies, waits for them, and re-layouts: 1.1 us -> none  [body(): lax.dynamic_index_in_dim(adjoint_start, even_layer, 2, keepdims=False)]
  transfers between devices with their start and end apart: 17 -> 9, of which waited for: 6 -> 5; matrix products, arithmetic and copies ran while one was open for 0% -> 0% of each run, Pallas kernels for 5% -> 12%
where the time goes in v3:
time: 47 us; the launch traced here: 46.7 us
  starting transfers between devices  24.5 us (52%)
  blocking collectives  9.44 us (20%)
  Pallas kernels  7.33 us (16%)
  waiting for transfers between devices  3.4 us (7%)
  between operations  0.77 us (2%)
  local copies, waits for them, and re-layouts  0.65 us (1%)
  other arithmetic  0.6 us (1%)
    ppermute x4, starting transfers between devices, odd_swap(): return lax.ppermute(layer, 'blocks', odd_pairs)  14 us
    ppermute x4, starting transfers between devices, even_swap(): return lax.ppermute(layer, 'blocks', even_pairs)  10.5 us
    all_gather x4, blocking collectives, cores(): return lax.all_gather(values, 'inst', axis=0)  9.44 us
    pallas_call x19, Pallas kernels, call(): pl.pallas_call(kernel, out_shape=[jax.ShapeDtypeStruct(s, jnp.float32) fo...  7.33 us
    ppermute x4, waiting for transfers between devices, even_swap(): return lax.ppermute(layer, 'blocks', even_pairs)  1.62 us
    ppermute x4, waiting for transfers between devices, odd_swap(): return lax.ppermute(layer, 'blocks', odd_pairs)  1.48 us
  transfers between devices with their start and end apart: 9, of which 5 were waited for; matrix products, arithmetic and copies ran while one was open for 0% of the time, Pallas kernels for 12%

profile of v3, /device:TPU:0, one launch (start us, length us, event | category | flops | bytes accessed | tf_op | source)
XLA Modules:
  0.0 46.7 jit_solution(1482425420236896367)
XLA Ops:
  0.6 1.0 %shard_map.77.after.even = f32[8,6,8,128]{3,2,1,0:T(8,128)S(1)} custom-call(f32[8,6,2,8,128]{4,3,2,1,0:T(8,128)} %source.3), custom_call_target="tpu_custom_call" | custom-call | flops 10000000000 | bytes 100000000 | tf_op jit(solution)/shard_map/pallas_call | solution.py:132
  1.6 3.0 %collective-permute-start = (f32[8,6,8,128]{3,2,1,0:T(8,128)S(1)}, f32[8,6,8,128]{3,2,1,0:T(8,128)S(1)}, u32[]{:S(2)}, u32[]{:S(2)}) collective-permute-start(f32[8,6,8,128]{3,2,1,0:T(8,128)S(1)} %shard_map.77.after.even), channel_id=1, source_target_pairs={{0,2},{2,0},{4,6},{6,4},{8,10},{10,8},{12,14},{14,12},{1,3},{3,1},... | collective-permute-start | bytes 589832 | tf_op jit(solution)/shard_map/ppermute | solution.py:202
  4.6 2.1 %shard_map.78 = (f32[8,6,2,8,128]{4,3,2,1,0:T(8,128)S(1)}, f32[8,6,6,2,8,128]{5,4,3,2,1,0:T(8,128)S(1)}, f32[8,6,2,8,128]{4,3,2,1,0:T(8,128)S(1)}, f32[8,6,8,128]{3,2,1,0:T(8,128)S(1)}) custom-call(f32[8,6,2,8,128]{4,3,2,1,0:T(8,128)} %grad.1, f32[8,6,6,2,8,128]{5,4,3,2,1,0:T(8,128)} %diag.1, f32[8,6,2,8,128]{4,3,2,1,0:T(8,128)} %coupling.1, ...), custom_call_target="tpu_custom_call" | custom-call | flops 10000000000 | bytes 100000000 | tf_op jit(solution)/shard_map/pallas_call | solution.py:132
  6.8 3.6 %collective-permute-start.1 = (f32[8,6,8,128]{3,2,1,0:T(8,128)S(1)}, f32[8,6,8,128]{3,2,1,0:T(8,128)S(1)}, u32[]{:S(2)}, u32[]{:S(2)}) collective-permute-start(f32[8,6,8,128]{3,2,1,0:T(8,128)S(1)} %get-tuple-element.10.odd), channel_id=1, source_target_pairs={{0,14},{2,4},{4,2},{6,8},{8,6},{10,12},{12,10},{14,0},{1,15},{3,5}... | collective-permute-start | bytes 589832 | tf_op jit(solution)/shard_map/ppermute | solution.py:205
  10.4 2.4 %all-gather = f32[4,8,6,8,128]{4,3,2,1,0:T(8,128)S(1)} all-gather(f32[2,8,6,8,128]{4,3,2,1,0:T(8,128)S(1)} %shard_map.79), channel_id=2, replica_groups=mesh['groups'=2,'blocks'=8,'inst'=2] {'inst'}, dimensions={0}, use_global_device_ids=true | all-gather | bytes 1179648 | tf_op jit(solution)/shard_map/all_gather | solution.py:208
  12.8 0.2 shard_map.80.base
  13.0 0.0 collective-permute-done.halo
  13.1 0.1 shard_map.81.refs_0_.even
  13.2 2.4 %collective-permute-start.2 = (f32[8,6,8,128]{3,2,1,0:T(8,128)S(1)}, f32[8,6,8,128]{3,2,1,0:T(8,128)S(1)}, u32[]{:S(2)}, u32[]{:S(2)}) collective-permute-start(f32[8,6,8,128]{3,2,1,0:T(8,128)S(1)} %shard_map.81.refs_0_.even), channel_id=1, source_target_pairs={{0,2},{2,0},{4,6},{6,4},{8,10},{10,8},{12,14},{14,12},{1,3},{3,1},... | collective-permute-start | bytes 589832 | tf_op jit(solution)/shard_map/ppermute | solution.py:202
  15.6 0.2 collective-permute-done.1.halo
  15.9 0.3 shard_map.82.odd
  16.3 3.8 %collective-permute-start.3 = (f32[8,6,8,128]{3,2,1,0:T(8,128)S(1)}, f32[8,6,8,128]{3,2,1,0:T(8,128)S(1)}, u32[]{:S(2)}, u32[]{:S(2)}) collective-permute-start(f32[8,6,8,128]{3,2,1,0:T(8,128)S(1)} %shard_map.82.odd), channel_id=1, source_target_pairs={{0,14},{2,4},{4,2},{6,8},{8,6},{10,12},{12,10},{14,0},{1,15},{3,5}... | collective-permute-start | bytes 589832 | tf_op jit(solution)/shard_map/ppermute | solution.py:205
  20.1 2.4 %all-gather.1 = f32[4,8,6,8,128]{4,3,2,1,0:T(8,128)S(1)} all-gather(f32[2,8,6,8,128]{4,3,2,1,0:T(8,128)S(1)} %shard_map.83), channel_id=3, replica_groups=mesh['groups'=2,'blocks'=8,'inst'=2] {'inst'}, dimensions={0}, use_global_device_ids=true | all-gather | bytes 1179648 | tf_op jit(solution)/shard_map/all_gather | solution.py:208
  22.4 0.2 shard_map.84.base
  22.7 0.3 collective-permute-done.2.halo
  23.0 0.1 shard_map.85.refs_0_.even
  23.1 2.5 %collective-permute-start.4 = (f32[8,6,8,128]{3,2,1,0:T(8,128)S(1)}, f32[8,6,8,128]{3,2,1,0:T(8,128)S(1)}, u32[]{:S(2)}, u32[]{:S(2)}) collective-permute-start(f32[8,6,8,128]{3,2,1,0:T(8,128)S(1)} %shard_map.85.refs_0_.even), channel_id=1, source_target_pairs={{0,2},{2,0},{4,6},{6,4},{8,10},{10,8},{12,14},{14,12},{1,3},{3,1},... | collective-permute-start | bytes 589832 | tf_op jit(solution)/shard_map/ppermute | solution.py:202
  25.6 0.0 collective-permute-done.3.halo
  25.6 0.3 shard_map.86.odd
  26.0 2.9 %collective-permute-start.5 = (f32[8,6,8,128]{3,2,1,0:T(8,128)S(1)}, f32[8,6,8,128]{3,2,1,0:T(8,128)S(1)}, u32[]{:S(2)}, u32[]{:S(2)}) collective-permute-start(f32[8,6,8,128]{3,2,1,0:T(8,128)S(1)} %shard_map.86.odd), channel_id=1, source_target_pairs={{0,14},{2,4},{4,2},{6,8},{8,6},{10,12},{12,10},{14,0},{1,15},{3,5}... | collective-permute-start | bytes 589832 | tf_op jit(solution)/shard_map/ppermute | solution.py:205
  28.9 2.4 %all-gather.2 = f32[4,8,6,8,128]{4,3,2,1,0:T(8,128)S(1)} all-gather(f32[2,8,6,8,128]{4,3,2,1,0:T(8,128)S(1)} %shard_map.87), channel_id=4, replica_groups=mesh['groups'=2,'blocks'=8,'inst'=2] {'inst'}, dimensions={0}, use_global_device_ids=true | all-gather | bytes 1179648 | tf_op jit(solution)/shard_map/all_gather | solution.py:208
  31.3 0.2 shard_map.88.base
  31.5 1.3 %collective-permute-done.4.halo = f32[8,6,8,128]{3,2,1,0:T(8,128)S(1)} collective-permute-done((f32[8,6,8,128]{3,2,1,0:T(8,128)S(1)}, f32[8,6,8,128]{3,2,1,0:T(8,128)S(1)}, u32[]{:S(2)}, u32[]{:S(2)}) %collective-permute-start.4) | collective-permute-done | bytes 196640 | tf_op jit(solution)/shard_map/ppermute | solution.py:202
  32.8 0.1 shard_map.89.refs_0_.even
  33.0 2.5 %collective-permute-start.6 = (f32[8,6,8,128]{3,2,1,0:T(8,128)S(1)}, f32[8,6,8,128]{3,2,1,0:T(8,128)S(1)}, u32[]{:S(2)}, u32[]{:S(2)}) collective-permute-start(f32[8,6,8,128]{3,2,1,0:T(8,128)S(1)} %shard_map.89.refs_0_.even), channel_id=1, source_target_pairs={{0,2},{2,0},{4,6},{6,4},{8,10},{10,8},{12,14},{14,12},{1,3},{3,1},... | collective-permute-start | bytes 589832 | tf_op jit(solution)/shard_map/ppermute | solution.py:202
  35.5 0.0 collective-permute-done.5.halo
  35.5 0.3 shard_map.90.odd
  35.9 3.6 %collective-permute-start.7 = (f32[8,6,8,128]{3,2,1,0:T(8,128)S(1)}, f32[8,6,8,128]{3,2,1,0:T(8,128)S(1)}, u32[]{:S(2)}, u32[]{:S(2)}) collective-permute-start(f32[8,6,8,128]{3,2,1,0:T(8,128)S(1)} %shard_map.90.odd), channel_id=1, source_target_pairs={{0,14},{2,4},{4,2},{6,8},{8,6},{10,12},{12,10},{14,0},{1,15},{3,5}... | collective-permute-start | bytes 589832 | tf_op jit(solution)/shard_map/ppermute | solution.py:205
  39.5 2.4 %all-gather.3 = f32[4,8,6,8,128]{4,3,2,1,0:T(8,128)S(1)} all-gather(f32[2,8,6,8,128]{4,3,2,1,0:T(8,128)S(1)} %shard_map.91), channel_id=5, replica_groups=mesh['groups'=2,'blocks'=8,'inst'=2] {'inst'}, dimensions={0}, use_global_device_ids=true | all-gather | bytes 1179648 | tf_op jit(solution)/shard_map/all_gather | solution.py:208
  41.9 0.0 copy-start
  41.9 0.0 copy-start.1
  41.9 0.3 shard_map.92.base
  42.1 0.0 collective-permute-done.6.halo
  42.1 0.6 %copy-done = f32[8,3,6,256]{3,0,2,1:T(8,128)S(1)} copy-done((f32[8,3,6,256]{3,0,2,1:T(8,128)S(1)}, f32[8,3,6,256]{3,0,2,1:T(8,128)}, u32[]{:S(2)}) %copy-start) | copy-done | bytes 147480
  42.8 0.0 copy-done.1
  42.8 0.3 shard_map.93
  43.1 1.2 %collective-permute-done.7.halo = f32[8,6,8,128]{3,2,1,0:T(8,128)S(1)} collective-permute-done((f32[8,6,8,128]{3,2,1,0:T(8,128)S(1)}, f32[8,6,8,128]{3,2,1,0:T(8,128)S(1)}, u32[]{:S(2)}, u32[]{:S(2)}) %collective-permute-start.7) | collective-permute-done | bytes 196640 | tf_op jit(solution)/shard_map/ppermute | solution.py:205
  44.3 0.6 %shard_map.94 = (f32[8,6,8,128]{3,2,1,0:T(8,128)S(1)}, f32[3,256]{1,0:T(4,128)S(1)}) custom-call(f32[8,6,8,128]{3,2,1,0:T(8,128)S(1)} %shard_map.90.odd, f32[2,2,8,6,8,128]{5,4,3,2,1,0:T(8,128)S(1)} %bitcast.7, f32[8,6,8,128]{3,2,1,0:T(8,128)S(1)} %shard_map.89.refs_0_.even, f32[8,6,8,128]{3,2,1,0:T(8,128)S(1)} %collective-permute-done.7.halo, ...), custom_call_target="tpu_custom_call" | custom-call | flops 10000000000 | bytes 100000000 | tf_op jit(solution)/shard_map/pallas_call | solution.py:132
  44.9 0.1 collective-permute-start.8
  45.0 0.9 %shard_map.95 = f32[8,6,2,8,128]{4,3,2,1,0:T(8,128)} custom-call(f32[8,6,8,128]{3,2,1,0:T(8,128)S(1)} %get-tuple-element.14.even, f32[8,6,8,128]{3,2,1,0:T(8,128)S(1)} %get-tuple-element.16.odd), custom_call_target="tpu_custom_call" | custom-call | flops 10000000000 | bytes 100000000 | tf_op jit(solution)/shard_map/pallas_call | solution.py:132
  45.8 0.3 collective-permute-done.8
  46.1 0.6 %add.3 = f32[3,256]{1,0:T(4,128)} add(f32[3,256]{1,0:T(4,128)S(1)} %get-tuple-element.17, f32[3,256]{1,0:T(4,128)S(1)} %collective-permute-done.8) | non-fusion elementwise | flops 768 | bytes 9216 | tf_op jit(solution)/shard_map/add | solution.py:248
  (4 shorter events, 0.1 us)
Async XLA Ops:
  1.6 11.4 %collective-permute-start = (f32[8,6,8,128]{3,2,1,0:T(8,128)S(1)}, f32[8,6,8,128]{3,2,1,0:T(8,128)S(1)}, u32[]{:S(2)}, u32[]{:S(2)}) collective-permute-start(f32[8,6,8,128]{3,2,1,0:T(8,128)S(1)} %shard_map.77.after.even), channel_id=1, source_target_pairs={{0,2},{2,0},{4,6},{6,4},{8,10},{10,8},{12,14},{14,12},{1,3},{3,1},... | collective-permute-start | bytes 589832 | tf_op jit(solution)/shard_map/ppermute | solution.py:202
  6.8 9.1 %collective-permute-start.1 = (f32[8,6,8,128]{3,2,1,0:T(8,128)S(1)}, f32[8,6,8,128]{3,2,1,0:T(8,128)S(1)}, u32[]{:S(2)}, u32[]{:S(2)}) collective-permute-start(f32[8,6,8,128]{3,2,1,0:T(8,128)S(1)} %get-tuple-element.10.odd), channel_id=1, source_target_pairs={{0,14},{2,4},{4,2},{6,8},{8,6},{10,12},{12,10},{14,0},{1,15},{3,5}... | collective-permute-start | bytes 589832 | tf_op jit(solution)/shard_map/ppermute | solution.py:205
  13.2 9.8 %collective-permute-start.2 = (f32[8,6,8,128]{3,2,1,0:T(8,128)S(1)}, f32[8,6,8,128]{3,2,1,0:T(8,128)S(1)}, u32[]{:S(2)}, u32[]{:S(2)}) collective-permute-start(f32[8,6,8,128]{3,2,1,0:T(8,128)S(1)} %shard_map.81.refs_0_.even), channel_id=1, source_target_pairs={{0,2},{2,0},{4,6},{6,4},{8,10},{10,8},{12,14},{14,12},{1,3},{3,1},... | collective-permute-start | bytes 589832 | tf_op jit(solution)/shard_map/ppermute | solution.py:202
  16.3 9.4 %collective-permute-start.3 = (f32[8,6,8,128]{3,2,1,0:T(8,128)S(1)}, f32[8,6,8,128]{3,2,1,0:T(8,128)S(1)}, u32[]{:S(2)}, u32[]{:S(2)}) collective-permute-start(f32[8,6,8,128]{3,2,1,0:T(8,128)S(1)} %shard_map.82.odd), channel_id=1, source_target_pairs={{0,14},{2,4},{4,2},{6,8},{8,6},{10,12},{12,10},{14,0},{1,15},{3,5}... | collective-permute-start | bytes 589832 | tf_op jit(solution)/shard_map/ppermute | solution.py:205
  23.1 9.7 %collective-permute-start.4 = (f32[8,6,8,128]{3,2,1,0:T(8,128)S(1)}, f32[8,6,8,128]{3,2,1,0:T(8,128)S(1)}, u32[]{:S(2)}, u32[]{:S(2)}) collective-permute-start(f32[8,6,8,128]{3,2,1,0:T(8,128)S(1)} %shard_map.85.refs_0_.even), channel_id=1, source_target_pairs={{0,2},{2,0},{4,6},{6,4},{8,10},{10,8},{12,14},{14,12},{1,3},{3,1},... | collective-permute-start | bytes 589832 | tf_op jit(solution)/shard_map/ppermute | solution.py:202
  26.0 9.5 %collective-permute-start.5 = (f32[8,6,8,128]{3,2,1,0:T(8,128)S(1)}, f32[8,6,8,128]{3,2,1,0:T(8,128)S(1)}, u32[]{:S(2)}, u32[]{:S(2)}) collective-permute-start(f32[8,6,8,128]{3,2,1,0:T(8,128)S(1)} %shard_map.86.odd), channel_id=1, source_target_pairs={{0,14},{2,4},{4,2},{6,8},{8,6},{10,12},{12,10},{14,0},{1,15},{3,5}... | collective-permute-start | bytes 589832 | tf_op jit(solution)/shard_map/ppermute | solution.py:205
  33.0 9.2 %collective-permute-start.6 = (f32[8,6,8,128]{3,2,1,0:T(8,128)S(1)}, f32[8,6,8,128]{3,2,1,0:T(8,128)S(1)}, u32[]{:S(2)}, u32[]{:S(2)}) collective-permute-start(f32[8,6,8,128]{3,2,1,0:T(8,128)S(1)} %shard_map.89.refs_0_.even), channel_id=1, source_target_pairs={{0,2},{2,0},{4,6},{6,4},{8,10},{10,8},{12,14},{14,12},{1,3},{3,1},... | collective-permute-start | bytes 589832 | tf_op jit(solution)/shard_map/ppermute | solution.py:202
  35.9 8.4 %collective-permute-start.7 = (f32[8,6,8,128]{3,2,1,0:T(8,128)S(1)}, f32[8,6,8,128]{3,2,1,0:T(8,128)S(1)}, u32[]{:S(2)}, u32[]{:S(2)}) collective-permute-start(f32[8,6,8,128]{3,2,1,0:T(8,128)S(1)} %shard_map.90.odd), channel_id=1, source_target_pairs={{0,14},{2,4},{4,2},{6,8},{8,6},{10,12},{12,10},{14,0},{1,15},{3,5}... | collective-permute-start | bytes 589832 | tf_op jit(solution)/shard_map/ppermute | solution.py:205
  41.9 0.9 %copy-start = (f32[8,3,6,256]{3,0,2,1:T(8,128)S(1)}, f32[8,3,6,256]{3,0,2,1:T(8,128)}, u32[]{:S(2)}) copy-start(f32[8,3,6,256]{3,0,2,1:T(8,128)} %param.11) | copy-start | bytes 442372
  41.9 0.9 %copy-start.1 = (s32[256]{0:T(256)S(1)}, s32[256]{0:T(256)}, u32[]{:S(2)}) copy-start(s32[256]{0:T(256)} %param.10) | copy-start | bytes 3076
  44.9 1.2 %collective-permute-start.8 = (f32[3,256]{1,0:T(4,128)S(1)}, f32[3,256]{1,0:T(4,128)S(1)}, u32[]{:S(2)}, u32[]{:S(2)}) collective-permute-start(f32[3,256]{1,0:T(4,128)S(1)} %get-tuple-element.17), channel_id=1, source_target_pairs={{0,1},{1,0},{2,3},{3,2},{4,5},{5,4},{6,7},{7,6},{8,9},{9,8},{10,11... | collective-permute-start | bytes 9224 | tf_op jit(solution)/shard_map/ppermute | solution.py:248

commit v4 on v3

--- a/solution.py
+++ b/solution.py
@@ -1,3 +1,4 @@
+import functools
 import math
 
 import jax
@@ -140,50 +141,43 @@
     )(*operands)
 
 
-def local_kernel(even, odd, both, grad, coupling, base, masked):
-    partner = both.at[1 - lax.axis_index("inst"), 0]
-    local_terms(own_layer(0), even, partner, odd, grad, coupling, base, masked)
-
-
-def even_layer(base, halo, fixed, last=None):
+def local_kernel(side, own, inner, both, grad, coupling, *refs):
+    base, masked = refs[-2:]
+    partner = both.at[1 - lax.axis_index("inst"), side]
+    local_terms(own_layer(side), own, partner, inner, grad, coupling, base, masked)
+
+
+def finish_layer(side, base, halo, fixed, last=None):
     _, diag, coupling = fixed
 
     def kernel(base, halo, diag, coupling, *refs):
-        layer = own_layer(0)
+        layer = own_layer(side)
         if last is None:
             (new,) = refs
         else:
-            index, partials, new, sens = refs
+            index, partials, *before, new, sens = refs
         update_layer(layer, base, halo, diag, coupling, new)
         if last is not None:
             for k, row in enumerate(layer_sensitivity(layer, new, index, partials)):
-                sens[k : k + 1, :] = row
+                sens[k : k + 1, :] = before[0][k : k + 1, :] + row if before else row
 
     operands = (base, halo, diag, coupling, *(last or ()))
     shapes = [base.shape] + ([] if last is None else [(last[1].shape[0], last[0].shape[1])])
     return call(kernel, shapes, [VMEM] * len(operands), operands)
 
 
-def odd_layer(odd, both, even, halo, fixed, after=(), last=None):
+def odd_layer(odd, both, even, halo, fixed, after):
     def kernel(odd, both, even, halo, grad, diag, coupling, *refs):
-        *refs, masked, base = refs[len(after) :]
+        new, masked, base = refs[len(after) :]
         layer = own_layer(1)
         partner = both.at[1 - lax.axis_index("inst"), 1]
-        if last is None:
-            (new,) = refs
-        else:
-            index, partials, before, new, sens = refs
         local_terms(layer, odd, partner, even, grad, coupling, base, masked)
         update_layer(layer, base, halo, diag, coupling, new)
-        if last is not None:
-            for k, row in enumerate(layer_sensitivity(layer, new, index, partials)):
-                sens[k : k + 1, :] = before[k : k + 1, :] + row
-
-    operands = (odd, both, even, halo, *fixed, *after, *(last or ()))
+
+    operands = (odd, both, even, halo, *fixed, *after)
     inst, _, radial, axial = odd.shape
-    shapes = [odd.shape] + ([] if last is None else [last[2].shape])
     scratch = [pltpu.VMEM((inst, 4, radial, axial), jnp.float32), pltpu.VMEM(odd.shape, jnp.float32)]
-    return call(kernel, shapes, [VMEM] * len(operands), operands, scratch)
+    return call(kernel, [odd.shape], [VMEM] * len(operands), operands, scratch)
 
 
 def body(
@@ -213,10 +207,10 @@
     def exchange(even, odd):
         return cores(*call(pack_kernel, [(2,) + shape], [VMEM] * 2, [even, odd]))
 
-    def local(even, odd, both):
-        operands = (even, odd, both, fixed[0], fixed[2])
+    def local(side, own, inner, both, after=()):
+        operands = (own, inner, both, fixed[0], fixed[2], *after)
         masked = pltpu.VMEM((inst, 4, radial, axial), jnp.float32)
-        return call(local_kernel, [shape], [VMEM] * 5, operands, [masked])[0]
+        return call(functools.partial(local_kernel, side), [shape], [VMEM] * len(operands), operands, [masked])[0]
 
     copies = [pltpu.SemaphoreType.DMA((inst + 3,))]
     start = in_hbm(adjoint_start)
@@ -233,17 +227,18 @@
     odd_halo = odd_swap(odd)
     both = exchange(even, odd)
     for sweep in range(SWEEPS - 1):
-        base = local(even, odd, both)
-        (new_even,) = even_layer(base, even_halo, fixed)
+        base = local(0, even, odd, both)
+        (new_even,) = finish_layer(0, base, even_halo, fixed)
         even_halo = even_swap(new_even)
         (odd,) = odd_layer(odd, both, even, odd_halo, fixed, [new_even])
         odd_halo = odd_swap(odd)
         even = new_even
         both = exchange(even, odd)
     last = index, partials
-    new_even, sens = even_layer(local(even, odd, both), even_halo, fixed, last)
-    odd, sens = odd_layer(odd, both, even, odd_halo, fixed, (), last + (sens,))
+    new_even, sens = finish_layer(0, local(0, even, odd, both), even_halo, fixed, last)
+    odd_base = local(1, odd, even, both, [new_even])
     even = new_even
+    odd, sens = finish_layer(1, odd_base, odd_halo, fixed, last + (sens,))
     (adjoint,) = call(join_kernel, [adjoint_start.shape], [VMEM] * 2, [even, odd], copies, HBM)
     return adjoint, sens + lax.ppermute(sens, "inst", [(0, 1), (1, 0)])
 

time: 47 us -> 46.7 us (level)
    pallas_call x19 -> x20, Pallas kernels: 7.33 us -> 7.31 us  [call(): pl.pallas_call(kernel, out_shape=[jax.ShapeDtypeStruct(s, jnp.float32) fo...]
  transfers between devices with their start and end apart: 9 -> 9, of which waited for: 5 -> 5; matrix products, arithmetic and copies ran while one was open for 0% -> 0% of each run, Pallas kernels for 12% -> 13%
where the time goes in v4:
time: 46.7 us; the launch traced here: 46.4 us
  starting transfers between devices  24.5 us (52%)
  blocking collectives  9.44 us (20%)
  Pallas kernels  7.31 us (16%)
  waiting for transfers between devices  3.14 us (7%)
  between operations  0.78 us (2%)
  local copies, waits for them, and re-layouts  0.65 us (1%)
  other arithmetic  0.6 us (1%)
    ppermute x4, starting transfers between devices, odd_swap(): return lax.ppermute(layer, 'blocks', odd_pairs)  14 us
    ppermute x4, starting transfers between devices, even_swap(): return lax.ppermute(layer, 'blocks', even_pairs)  10.5 us
    all_gather x4, blocking collectives, cores(): return lax.all_gather(values, 'inst', axis=0)  9.44 us
    pallas_call x20, Pallas kernels, call(): pl.pallas_call(kernel, out_shape=[jax.ShapeDtypeStruct(s, jnp.float32) fo...  7.31 us
    ppermute x4, waiting for transfers between devices, even_swap(): return lax.ppermute(layer, 'blocks', even_pairs)  1.62 us
    ppermute x4, waiting for transfers between devices, odd_swap(): return lax.ppermute(layer, 'blocks', odd_pairs)  1.23 us
  transfers between devices with their start and end apart: 9, of which 5 were waited for; matrix products, arithmetic and copies ran while one was open for 0% of the time, Pallas kernels for 13%

profile of v4, /device:TPU:0, one launch (start us, length us, event | category | flops | bytes accessed | tf_op | source)
XLA Modules:
  0.0 46.4 jit_solution(5267132400136212342)
XLA Ops:
  0.6 1.0 %shard_map.77.after.even.own = f32[8,6,8,128]{3,2,1,0:T(8,128)S(1)} custom-call(f32[8,6,2,8,128]{4,3,2,1,0:T(8,128)} %source.3), custom_call_target="tpu_custom_call" | custom-call | flops 10000000000 | bytes 100000000 | tf_op jit(solution)/shard_map/pallas_call | solution.py:133
  1.6 3.0 %collective-permute-start = (f32[8,6,8,128]{3,2,1,0:T(8,128)S(1)}, f32[8,6,8,128]{3,2,1,0:T(8,128)S(1)}, u32[]{:S(2)}, u32[]{:S(2)}) collective-permute-start(f32[8,6,8,128]{3,2,1,0:T(8,128)S(1)} %shard_map.77.after.even.own), channel_id=1, source_target_pairs={{0,2},{2,0},{4,6},{6,4},{8,10},{10,8},{12,14},{14,12},{1,3},{3,1},... | collective-permute-start | bytes 589832 | tf_op jit(solution)/shard_map/ppermute | solution.py:196
  4.6 2.1 %shard_map.78 = (f32[8,6,2,8,128]{4,3,2,1,0:T(8,128)S(1)}, f32[8,6,6,2,8,128]{5,4,3,2,1,0:T(8,128)S(1)}, f32[8,6,2,8,128]{4,3,2,1,0:T(8,128)S(1)}, f32[8,6,8,128]{3,2,1,0:T(8,128)S(1)}) custom-call(f32[8,6,2,8,128]{4,3,2,1,0:T(8,128)} %grad.1, f32[8,6,6,2,8,128]{5,4,3,2,1,0:T(8,128)} %diag.1, f32[8,6,2,8,128]{4,3,2,1,0:T(8,128)} %coupling.1, ...), custom_call_target="tpu_custom_call" | custom-call | flops 10000000000 | bytes 100000000 | tf_op jit(solution)/shard_map/pallas_call | solution.py:133
  6.8 3.6 %collective-permute-start.1 = (f32[8,6,8,128]{3,2,1,0:T(8,128)S(1)}, f32[8,6,8,128]{3,2,1,0:T(8,128)S(1)}, u32[]{:S(2)}, u32[]{:S(2)}) collective-permute-start(f32[8,6,8,128]{3,2,1,0:T(8,128)S(1)} %get-tuple-element.10.odd.inner), channel_id=1, source_target_pairs={{0,14},{2,4},{4,2},{6,8},{8,6},{10,12},{12,10},{14,0},{1,15},{3,5}... | collective-permute-start | bytes 589832 | tf_op jit(solution)/shard_map/ppermute | solution.py:199
  10.4 2.4 %all-gather = f32[4,8,6,8,128]{4,3,2,1,0:T(8,128)S(1)} all-gather(f32[2,8,6,8,128]{4,3,2,1,0:T(8,128)S(1)} %shard_map.79), channel_id=2, replica_groups=mesh['groups'=2,'blocks'=8,'inst'=2] {'inst'}, dimensions={0}, use_global_device_ids=true | all-gather | bytes 1179648 | tf_op jit(solution)/shard_map/all_gather | solution.py:202
  12.8 0.2 shard_map.80.base
  13.0 0.0 collective-permute-done.halo
  13.1 0.1 shard_map.81.refs_0_.even.own
  13.2 2.4 %collective-permute-start.2 = (f32[8,6,8,128]{3,2,1,0:T(8,128)S(1)}, f32[8,6,8,128]{3,2,1,0:T(8,128)S(1)}, u32[]{:S(2)}, u32[]{:S(2)}) collective-permute-start(f32[8,6,8,128]{3,2,1,0:T(8,128)S(1)} %shard_map.81.refs_0_.even.own), channel_id=1, source_target_pairs={{0,2},{2,0},{4,6},{6,4},{8,10},{10,8},{12,14},{14,12},{1,3},{3,1},... | collective-permute-start | bytes 589832 | tf_op jit(solution)/shard_map/ppermute | solution.py:196
  15.6 0.2 collective-permute-done.1.halo
  15.9 0.3 shard_map.82.odd.inner
  16.3 3.8 %collective-permute-start.3 = (f32[8,6,8,128]{3,2,1,0:T(8,128)S(1)}, f32[8,6,8,128]{3,2,1,0:T(8,128)S(1)}, u32[]{:S(2)}, u32[]{:S(2)}) collective-permute-start(f32[8,6,8,128]{3,2,1,0:T(8,128)S(1)} %shard_map.82.odd.inner), channel_id=1, source_target_pairs={{0,14},{2,4},{4,2},{6,8},{8,6},{10,12},{12,10},{14,0},{1,15},{3,5}... | collective-permute-start | bytes 589832 | tf_op jit(solution)/shard_map/ppermute | solution.py:199
  20.1 2.4 %all-gather.1 = f32[4,8,6,8,128]{4,3,2,1,0:T(8,128)S(1)} all-gather(f32[2,8,6,8,128]{4,3,2,1,0:T(8,128)S(1)} %shard_map.83), channel_id=3, replica_groups=mesh['groups'=2,'blocks'=8,'inst'=2] {'inst'}, dimensions={0}, use_global_device_ids=true | all-gather | bytes 1179648 | tf_op jit(solution)/shard_map/all_gather | solution.py:202
  22.4 0.2 shard_map.84.base
  22.7 0.3 collective-permute-done.2.halo
  23.0 0.1 shard_map.85.refs_0_.even.own
  23.1 2.5 %collective-permute-start.4 = (f32[8,6,8,128]{3,2,1,0:T(8,128)S(1)}, f32[8,6,8,128]{3,2,1,0:T(8,128)S(1)}, u32[]{:S(2)}, u32[]{:S(2)}) collective-permute-start(f32[8,6,8,128]{3,2,1,0:T(8,128)S(1)} %shard_map.85.refs_0_.even.own), channel_id=1, source_target_pairs={{0,2},{2,0},{4,6},{6,4},{8,10},{10,8},{12,14},{14,12},{1,3},{3,1},... | collective-permute-start | bytes 589832 | tf_op jit(solution)/shard_map/ppermute | solution.py:196
  25.6 0.0 collective-permute-done.3.halo
  25.6 0.3 shard_map.86.odd.inner
  26.0 2.9 %collective-permute-start.5 = (f32[8,6,8,128]{3,2,1,0:T(8,128)S(1)}, f32[8,6,8,128]{3,2,1,0:T(8,128)S(1)}, u32[]{:S(2)}, u32[]{:S(2)}) collective-permute-start(f32[8,6,8,128]{3,2,1,0:T(8,128)S(1)} %shard_map.86.odd.inner), channel_id=1, source_target_pairs={{0,14},{2,4},{4,2},{6,8},{8,6},{10,12},{12,10},{14,0},{1,15},{3,5}... | collective-permute-start | bytes 589832 | tf_op jit(solution)/shard_map/ppermute | solution.py:199
  28.9 2.4 %all-gather.2 = f32[4,8,6,8,128]{4,3,2,1,0:T(8,128)S(1)} all-gather(f32[2,8,6,8,128]{4,3,2,1,0:T(8,128)S(1)} %shard_map.87), channel_id=4, replica_groups=mesh['groups'=2,'blocks'=8,'inst'=2] {'inst'}, dimensions={0}, use_global_device_ids=true | all-gather | bytes 1179648 | tf_op jit(solution)/shard_map/all_gather | solution.py:202
  31.3 0.2 shard_map.88.base
  31.5 1.3 %collective-permute-done.4.halo = f32[8,6,8,128]{3,2,1,0:T(8,128)S(1)} collective-permute-done((f32[8,6,8,128]{3,2,1,0:T(8,128)S(1)}, f32[8,6,8,128]{3,2,1,0:T(8,128)S(1)}, u32[]{:S(2)}, u32[]{:S(2)}) %collective-permute-start.4) | collective-permute-done | bytes 196640 | tf_op jit(solution)/shard_map/ppermute | solution.py:196
  32.8 0.1 shard_map.89.refs_0_.even.own.inner
  33.0 2.5 %collective-permute-start.6 = (f32[8,6,8,128]{3,2,1,0:T(8,128)S(1)}, f32[8,6,8,128]{3,2,1,0:T(8,128)S(1)}, u32[]{:S(2)}, u32[]{:S(2)}) collective-permute-start(f32[8,6,8,128]{3,2,1,0:T(8,128)S(1)} %shard_map.89.refs_0_.even.own.inner), channel_id=1, source_target_pairs={{0,2},{2,0},{4,6},{6,4},{8,10},{10,8},{12,14},{14,12},{1,3},{3,1},... | collective-permute-start | bytes 589832 | tf_op jit(solution)/shard_map/ppermute | solution.py:196
  35.5 0.0 collective-permute-done.5.halo
  35.5 0.3 shard_map.90.odd.inner.own
  35.9 3.6 %collective-permute-start.7 = (f32[8,6,8,128]{3,2,1,0:T(8,128)S(1)}, f32[8,6,8,128]{3,2,1,0:T(8,128)S(1)}, u32[]{:S(2)}, u32[]{:S(2)}) collective-permute-start(f32[8,6,8,128]{3,2,1,0:T(8,128)S(1)} %shard_map.90.odd.inner.own), channel_id=1, source_target_pairs={{0,14},{2,4},{4,2},{6,8},{8,6},{10,12},{12,10},{14,0},{1,15},{3,5}... | collective-permute-start | bytes 589832 | tf_op jit(solution)/shard_map/ppermute | solution.py:199
  39.5 2.4 %all-gather.3 = f32[4,8,6,8,128]{4,3,2,1,0:T(8,128)S(1)} all-gather(f32[2,8,6,8,128]{4,3,2,1,0:T(8,128)S(1)} %shard_map.91), channel_id=5, replica_groups=mesh['groups'=2,'blocks'=8,'inst'=2] {'inst'}, dimensions={0}, use_global_device_ids=true | all-gather | bytes 1179648 | tf_op jit(solution)/shard_map/all_gather | solution.py:202
  41.9 0.0 copy-start
  41.9 0.0 copy-start.1
  41.9 0.2 shard_map.92.base
  42.1 0.0 collective-permute-done.6.halo
  42.1 0.6 %copy-done = f32[8,3,6,256]{3,0,2,1:T(8,128)S(1)} copy-done((f32[8,3,6,256]{3,0,2,1:T(8,128)S(1)}, f32[8,3,6,256]{3,0,2,1:T(8,128)}, u32[]{:S(2)}) %copy-start) | copy-done | bytes 147480
  42.8 0.0 copy-done.1
  42.8 0.3 shard_map.93
  43.1 0.3 shard_map.94.base
  43.3 1.0 %collective-permute-done.7.halo = f32[8,6,8,128]{3,2,1,0:T(8,128)S(1)} collective-permute-done((f32[8,6,8,128]{3,2,1,0:T(8,128)S(1)}, f32[8,6,8,128]{3,2,1,0:T(8,128)S(1)}, u32[]{:S(2)}, u32[]{:S(2)}) %collective-permute-start.7) | collective-permute-done | bytes 196640 | tf_op jit(solution)/shard_map/ppermute | solution.py:199
  44.3 0.3 shard_map.95
  44.6 0.1 collective-permute-start.8
  44.7 0.9 %shard_map.96 = f32[8,6,2,8,128]{4,3,2,1,0:T(8,128)} custom-call(f32[8,6,8,128]{3,2,1,0:T(8,128)S(1)} %get-tuple-element.14.refs_0_.even, f32[8,6,8,128]{3,2,1,0:T(8,128)S(1)} %get-tuple-element.16.odd), custom_call_target="tpu_custom_call" | custom-call | flops 10000000000 | bytes 100000000 | tf_op jit(solution)/shard_map/pallas_call | solution.py:133
  45.5 0.3 collective-permute-done.8
  45.8 0.6 %add.3 = f32[3,256]{1,0:T(4,128)} add(f32[3,256]{1,0:T(4,128)S(1)} %get-tuple-element.17, f32[3,256]{1,0:T(4,128)S(1)} %collective-permute-done.8) | non-fusion elementwise | flops 768 | bytes 9216 | tf_op jit(solution)/shard_map/add | solution.py:243
  (4 shorter events, 0.1 us)
Async XLA Ops:
  1.6 11.4 %collective-permute-start = (f32[8,6,8,128]{3,2,1,0:T(8,128)S(1)}, f32[8,6,8,128]{3,2,1,0:T(8,128)S(1)}, u32[]{:S(2)}, u32[]{:S(2)}) collective-permute-start(f32[8,6,8,128]{3,2,1,0:T(8,128)S(1)} %shard_map.77.after.even.own), channel_id=1, source_target_pairs={{0,2},{2,0},{4,6},{6,4},{8,10},{10,8},{12,14},{14,12},{1,3},{3,1},... | collective-permute-start | bytes 589832 | tf_op jit(solution)/shard_map/ppermute | solution.py:196
  6.8 9.1 %collective-permute-start.1 = (f32[8,6,8,128]{3,2,1,0:T(8,128)S(1)}, f32[8,6,8,128]{3,2,1,0:T(8,128)S(1)}, u32[]{:S(2)}, u32[]{:S(2)}) collective-permute-start(f32[8,6,8,128]{3,2,1,0:T(8,128)S(1)} %get-tuple-element.10.odd.inner), channel_id=1, source_target_pairs={{0,14},{2,4},{4,2},{6,8},{8,6},{10,12},{12,10},{14,0},{1,15},{3,5}... | collective-permute-start | bytes 589832 | tf_op jit(solution)/shard_map/ppermute | solution.py:199
  13.2 9.8 %collective-permute-start.2 = (f32[8,6,8,128]{3,2,1,0:T(8,128)S(1)}, f32[8,6,8,128]{3,2,1,0:T(8,128)S(1)}, u32[]{:S(2)}, u32[]{:S(2)}) collective-permute-start(f32[8,6,8,128]{3,2,1,0:T(8,128)S(1)} %shard_map.81.refs_0_.even.own), channel_id=1, source_target_pairs={{0,2},{2,0},{4,6},{6,4},{8,10},{10,8},{12,14},{14,12},{1,3},{3,1},... | collective-permute-start | bytes 589832 | tf_op jit(solution)/shard_map/ppermute | solution.py:196
  16.3 9.4 %collective-permute-start.3 = (f32[8,6,8,128]{3,2,1,0:T(8,128)S(1)}, f32[8,6,8,128]{3,2,1,0:T(8,128)S(1)}, u32[]{:S(2)}, u32[]{:S(2)}) collective-permute-start(f32[8,6,8,128]{3,2,1,0:T(8,128)S(1)} %shard_map.82.odd.inner), channel_id=1, source_target_pairs={{0,14},{2,4},{4,2},{6,8},{8,6},{10,12},{12,10},{14,0},{1,15},{3,5}... | collective-permute-start | bytes 589832 | tf_op jit(solution)/shard_map/ppermute | solution.py:199
  23.1 9.7 %collective-permute-start.4 = (f32[8,6,8,128]{3,2,1,0:T(8,128)S(1)}, f32[8,6,8,128]{3,2,1,0:T(8,128)S(1)}, u32[]{:S(2)}, u32[]{:S(2)}) collective-permute-start(f32[8,6,8,128]{3,2,1,0:T(8,128)S(1)} %shard_map.85.refs_0_.even.own), channel_id=1, source_target_pairs={{0,2},{2,0},{4,6},{6,4},{8,10},{10,8},{12,14},{14,12},{1,3},{3,1},... | collective-permute-start | bytes 589832 | tf_op jit(solution)/shard_map/ppermute | solution.py:196
  26.0 9.5 %collective-permute-start.5 = (f32[8,6,8,128]{3,2,1,0:T(8,128)S(1)}, f32[8,6,8,128]{3,2,1,0:T(8,128)S(1)}, u32[]{:S(2)}, u32[]{:S(2)}) collective-permute-start(f32[8,6,8,128]{3,2,1,0:T(8,128)S(1)} %shard_map.86.odd.inner), channel_id=1, source_target_pairs={{0,14},{2,4},{4,2},{6,8},{8,6},{10,12},{12,10},{14,0},{1,15},{3,5}... | collective-permute-start | bytes 589832 | tf_op jit(solution)/shard_map/ppermute | solution.py:199
  33.0 9.2 %collective-permute-start.6 = (f32[8,6,8,128]{3,2,1,0:T(8,128)S(1)}, f32[8,6,8,128]{3,2,1,0:T(8,128)S(1)}, u32[]{:S(2)}, u32[]{:S(2)}) collective-permute-start(f32[8,6,8,128]{3,2,1,0:T(8,128)S(1)} %shard_map.89.refs_0_.even.own.inner), channel_id=1, source_target_pairs={{0,2},{2,0},{4,6},{6,4},{8,10},{10,8},{12,14},{14,12},{1,3},{3,1},... | collective-permute-start | bytes 589832 | tf_op jit(solution)/shard_map/ppermute | solution.py:196
  35.9 8.4 %collective-permute-start.7 = (f32[8,6,8,128]{3,2,1,0:T(8,128)S(1)}, f32[8,6,8,128]{3,2,1,0:T(8,128)S(1)}, u32[]{:S(2)}, u32[]{:S(2)}) collective-permute-start(f32[8,6,8,128]{3,2,1,0:T(8,128)S(1)} %shard_map.90.odd.inner.own), channel_id=1, source_target_pairs={{0,14},{2,4},{4,2},{6,8},{8,6},{10,12},{12,10},{14,0},{1,15},{3,5}... | collective-permute-start | bytes 589832 | tf_op jit(solution)/shard_map/ppermute | solution.py:199
  41.9 0.9 %copy-start = (f32[8,3,6,256]{3,0,2,1:T(8,128)S(1)}, f32[8,3,6,256]{3,0,2,1:T(8,128)}, u32[]{:S(2)}) copy-start(f32[8,3,6,256]{3,0,2,1:T(8,128)} %param.11) | copy-start | bytes 442372
  41.9 0.9 %copy-start.1 = (s32[256]{0:T(256)S(1)}, s32[256]{0:T(256)}, u32[]{:S(2)}) copy-start(s32[256]{0:T(256)} %param.10) | copy-start | bytes 3076
  44.6 1.2 %collective-permute-start.8 = (f32[3,256]{1,0:T(4,128)S(1)}, f32[3,256]{1,0:T(4,128)S(1)}, u32[]{:S(2)}, u32[]{:S(2)}) collective-permute-start(f32[3,256]{1,0:T(4,128)S(1)} %get-tuple-element.17), channel_id=1, source_target_pairs={{0,1},{1,0},{2,3},{3,2},{4,5},{5,4},{6,7},{7,6},{8,9},{9,8},{10,11... | collective-permute-start | bytes 9224 | tf_op jit(solution)/shard_map/ppermute | solution.py:243
